TPU v7x, 32 devices: a whole 2x2x4 slice. The times are simulated.
32 devices in a mesh: pb: 8 (over y, x, core), row: 4 (over z).
Axes of the slice: x: 2, y: 2, z: 4, core: 2. Of those that a mesh axis runs over, the one named last changes fastest.
Arguments:
- valence_bands: bfloat16 [8, 20, 4096], P('pb', None, 'row'), may hold values from -0.75 to 0.75
- conduction_bands: bfloat16 [8, 20, 4096], P('pb', None, 'row'), may hold values from -6 to 6
- screened: bfloat16 [8, 4096, 4096], P('pb', 'row'), may hold values from -0.09375 to 0.09375
- pair_list: int32 [16, 2], replicated, may hold values from 0 to 7, as said below
- transfer_index: int32 [16, 1], replicated, may hold values from 0 to 7; in each aligned block of 16 rows (0 to 15, 16 to 31, ...) at most 6 rows name the same one
- owner_map: int32 [8], replicated, may hold values from 0 to 7, as said below
Outputs:
- direct: bfloat16 [16, 400, 400], P('pb', 'row')
- mirror: bfloat16 [16, 400, 400], P('pb', 'row')
Inputs may be any that keep to these rules, and one draw needn't show every extreme that they name: owner_map is a permutation of 0 to 7. `pair_list`: the two k-points of a pair differ. The first k-point of pairs e * 2 to e * 2 + 1 is the one that owner_map sends to e. Over all pairs, the second k-points are sent by owner_map to every value 0 to 7 exactly 2 times. `transfer_index`: at most 6 pairs share one momentum transfer, and some transfer has exactly 6; every transfer has at least one pair.
All inputs are finite; a program needn't handle non-finite values.
Results may differ from a plain program's by a relative error of at most 0.0065.
Values may be sent and summed in bfloat16 or wider, within the bound.
No kernel may reach another device: no remote copies, remote signals or barrier semaphores. Data moves between devices by JAX's collectives and lax.ppermute only.
A program may use at most 64 MiB of HBM per device.

v0:
```python
import functools
import math

import jax
import jax.numpy as jnp
from jax import lax
from jax.experimental import pallas as pl
from jax.experimental.pallas import tpu as pltpu
from jax.sharding import PartitionSpec as P


PAIR_DEV = 2
MOST = 6
SUB = 8
F32, BF16, I32 = jnp.float32, jnp.bfloat16, jnp.int32
SMEM = pl.BlockSpec(memory_space=pltpu.SMEM)
VMEM = pl.BlockSpec(memory_space=pltpu.VMEM)
ANY = pl.BlockSpec(memory_space=pl.ANY)
LIVE, SWAP, FBIT, FIDX, SBIT, SIDX, ROW, DEEP = range(8)
GROUP = 2


def table_body(pairs, transfers, owners, slots_out, route_out, rank, count, *, slots, groups, rows_split):
    me = lax.axis_index("pb")
    row = lax.axis_index("row")
    total = pairs.shape[1]
    partner = me ^ 1
    for q in range(groups):
        count[q] = 0
    for p in range(total):
        q = transfers[p]
        rank[p] = count[q]
        count[q] = count[q] + 1
    for s in range(slots):
        for k in range(8):
            slots_out[s, k] = 0
        slots_out[s, ROW] = row
    deep = 0
    for q in range(0, groups, 2):
        deep = jnp.maximum(deep, (count[q] + count[q + 1] + 1) // 2)
    for s in range(slots):
        slots_out[s, DEEP] = deep

    def place(p):
        q = transfers[p]
        low = q & ~1
        pos = rank[p] + jnp.where(q == low, 0, count[low])
        half = (count[low] + count[low + 1] + 1) // 2
        core = (pos >= half).astype(I32)
        return q, low | core, pos - core * half

    wanted = {}
    for d, name in ((me, 0), (partner, 1)):
        for j in range(PAIR_DEV):
            wanted[name, j] = d * PAIR_DEV + j

    def put(name, t, p):
        _, source, slot = place(p)
        away = source ^ jnp.where(name == 0, me, partner)
        route_out[name, t, 0] = away & 1
        route_out[name, t, 1] = (away >> 1) * (-(-slots // GROUP) * GROUP) + slot

    for name in range(2):
        for j in range(PAIR_DEV):
            put(name, j, wanted[name, j])
    for k in range(2):
        count[groups + k] = 0
    for p in range(total):
        q, source, slot = place(p)
        first = owners[pairs[0, p]] ^ me
        second = owners[pairs[1, p]] ^ me

        @pl.when(source == me)
        def _(q=q, slot=slot, first=first, second=second):
            slots_out[slot, LIVE] = 1
            slots_out[slot, SWAP] = (q != me).astype(I32)
            slots_out[slot, FBIT] = first & 1
            slots_out[slot, FIDX] = first >> 1
            slots_out[slot, SBIT] = second & 1
            slots_out[slot, SIDX] = second >> 1

        for name, d in ((0, 0), (1, 1)):
            @pl.when(second == d)
            def _(name=name, p=p):
                k = count[groups + name]
                put(name, PAIR_DEV + k, p)
                count[groups + name] = k + 1


def tables(pair_list, transfer_index, owner_map, slots, groups, rows_split):
    body = functools.partial(table_body, slots=slots, groups=groups, rows_split=rows_split)
    return pl.pallas_call(
        body,
        out_shape=[
            jax.ShapeDtypeStruct((slots, 8), I32),
            jax.ShapeDtypeStruct((2, 2 * PAIR_DEV, 2), I32),
        ],
        in_specs=[SMEM] * 3,
        out_specs=[SMEM] * 2,
        scratch_shapes=[pltpu.SMEM((pair_list.shape[0],), I32), pltpu.SMEM((groups + 2,), I32)],
    )(pair_list.T, transfer_index.reshape(-1), owner_map)


def pair_body(info, own, own_rest, other, other_rest, w_own, w_other, *rest, slots, rows_split, parts, chunk):
    outs = rest[:rows_split]
    near, far, products, wbuf, interim, val_products, result, sem, con_sem = rest[rows_split:]
    nc = own.shape[1] // 2
    nloc = own.shape[2]
    m = w_own.shape[0]
    nv = nc
    per = nv // rows_split
    height = val_products.shape[0] // rows_split
    step = m // parts
    base = slots[0]
    row = info[base, ROW]

    def band_copies(i, which, bit):
        k = info[base + i, FIDX if which == 0 else SIDX]
        src, src_rest = (own, own_rest) if bit == 0 else (other, other_rest)
        return (
            pltpu.make_async_copy(src.at[k], near.at[i, which], con_sem.at[0, i, which]),
            pltpu.make_async_copy(src_rest.at[k], far.at[i, which], con_sem.at[1, i, which]),
        )

    def w_copy(which, k):
        rows = pl.ds(k * step, step)
        return pltpu.make_async_copy((w_own, w_other)[which].at[rows], wbuf.at[which, rows], sem.at[which, k])

    count = len(slots)
    live = [info[s, LIVE] != 0 for s in slots]
    for i in range(count):
        for which, flag in ((0, FBIT), (1, SBIT)):
            for bit in range(2):
                @pl.when(live[i] & (info[slots[i], flag] == bit))
                def _(i=i, which=which, bit=bit):
                    for c in band_copies(i, which, bit):
                        c.start()
        for which in range(2):
            new = live[i] & (info[slots[i], SWAP] == which)
            for before in range(i):
                new = new & ~(live[before] & (info[slots[before], SWAP] == which))

            @pl.when(new)
            def _(which=which):
                for k in range(parts):
                    w_copy(which, k).start()

    def lows(n):
        rows = lax.broadcasted_iota(I32, (SUB, n), 0)
        return {i: rows < i for i in range(1, SUB)}

    def tile(lines, tiled, at, total, width, low):
        n = tiled.shape[1]
        lo, hi = min(at, total - 1) // width, min(at + SUB - 1, total - 1) // width
        left = jnp.broadcast_to(lines[lo:lo + 1], (SUB, n))
        if hi != lo:
            left = jnp.where(low[hi * width - at], left, jnp.broadcast_to(lines[hi:hi + 1], (SUB, n)))
        start = at % tiled.shape[0]
        return left * tiled[start:start + SUB]

    group = 2 * SUB // math.gcd(nc, 2 * SUB)

    @pl.loop(0, count)
    def _(i):
        slot = base + i

        @pl.when(info[slot, LIVE] != 0)
        def _():
            for which in range(2):
                pltpu.make_async_copy(own.at[0], near.at[i, which], con_sem.at[0, i, which]).wait()
                pltpu.make_async_copy(own_rest.at[0], far.at[i, which], con_sem.at[1, i, which]).wait()
            low = lows(chunk)
            for j in range(rows_split):
                block = row ^ j
                for k in range(0, nloc, chunk):
                    def band(which):
                        if j == 0:
                            return near[i, which, :, k:k + chunk].astype(F32)[:nc]
                        return far[i, which, :, k:k + chunk].astype(F32)[(j - 1) * nc:j * nc]

                    lines = band(0)
                    tiled = jnp.concatenate([band(1)] * group, axis=0)
                    cols = pl.ds(pl.multiple_of(block * nloc + k, 128), chunk)
                    for at in range(0, nc * nc, 2 * SUB):
                        two = [tile(lines, tiled, at + o, nc * nc, nc, low) for o in (0, SUB)]
                        products[at:at + 2 * SUB, cols] = jnp.concatenate(two, axis=0).astype(BF16)

            low = lows(nloc)
            lines = near[i, 0].astype(F32)[nc:]
            tiled = jnp.concatenate([near[i, 1].astype(F32)[nc:]] * (per + 1), axis=0)
            for s in range(rows_split):
                for at in range(0, height, SUB):
                    x = tile(lines[s * per:(s + 1) * per], tiled, at, per * nv, nv, low)
                    val_products[s * height + at:s * height + at + SUB, :] = x.astype(BF16)

            swap = info[slot, SWAP]
            fresh = jnp.bool_(True)
            for before in range(count):
                used = live[before] & (info[slots[before], SWAP] == swap) & (before < i)
                fresh = fresh & ~used
            for k in range(parts):
                for which in range(2):
                    @pl.when(fresh & (swap == which))
                    def _(which=which, k=k):
                        w_copy(which, k).wait()
                got = lax.dot_general(
                    products[...], wbuf[swap, k * step:(k + 1) * step, :], (((1,), (1,)), ((), ())),
                    preferred_element_type=F32,
                )
                interim[:, k * step:(k + 1) * step] = got.astype(BF16)
            res = lax.dot_general(
                val_products[...], interim[...], (((1,), (1,)), ((), ())), preferred_element_type=F32
            )
            for s in range(rows_split):
                result[s] = res[s * height:(s + 1) * height]
            for g in range(count):
                @pl.when(i == g)
                def _(g=g):
                    for s in range(rows_split):
                        piece = result[row ^ s]
                        outs[s][:, g * nc * nc:(g + 1) * nc * nc] = piece[:per * nv].astype(BF16)


def pair_call(info, slots, own, own_rest, other, other_rest, w_own, w_other, rows_split, parts=2, chunk=256):
    nc = own.shape[1] // 2
    m, n = w_own.shape
    nv = nc
    per = nv // rows_split
    height = -(-per * nv // SUB) * SUB
    count = len(slots)
    return pl.pallas_call(
        functools.partial(pair_body, slots=slots, rows_split=rows_split, parts=parts, chunk=chunk),
        out_shape=[jax.ShapeDtypeStruct((per * nv, count * nc * nc), BF16)] * rows_split,
        in_specs=[SMEM] + [ANY] * 6,
        out_specs=[VMEM] * rows_split,
        scratch_shapes=[
            pltpu.VMEM((count, 2) + own.shape[1:], BF16),
            pltpu.VMEM((count, 2) + own_rest.shape[1:], BF16),
            pltpu.VMEM((nc * nc, n), BF16),
            pltpu.VMEM((2, m, n), BF16),
            pltpu.VMEM((nc * nc, m), BF16),
            pltpu.VMEM((rows_split * height, m), BF16),
            pltpu.VMEM((rows_split, height, nc * nc), F32),
            pltpu.SemaphoreType.DMA((2, parts)),
            pltpu.SemaphoreType.DMA((2, count, 2)),
        ],
        compiler_params=pltpu.CompilerParams(vmem_limit_bytes=60 << 20),
        cost_estimate=pl.CostEstimate(
            flops=2 * count * nc * nc * m * n, bytes_accessed=2 * m * n, transcendentals=0
        ),
    )(info, own, own_rest, other, other_rest, w_own, w_other)


def fetch(route, near, far, held, sem, wants):
    for i, t in enumerate(wants):
        code = route[0, t, 1]
        for bit, blocks in ((0, near), (1, far)):
            @pl.when(route[0, t, 0] == bit)
            def _(i=i, code=code, blocks=blocks):
                for k, block in enumerate(blocks):
                    @pl.when(code // GROUP == k)
                    def _(block=block):
                        pltpu.make_async_copy(block.at[code % GROUP], held.at[i], sem.at[i]).start()
    for i in range(len(wants)):
        pltpu.make_async_copy(near[0].at[0], held.at[i], sem.at[i]).wait()


def direct_body(route, *rest):
    blocks, direct, sem = rest[:-2], rest[-2], rest[-1]
    half = len(blocks) // 2
    fetch(route, blocks[:half], blocks[half:], direct, sem, range(PAIR_DEV))


def direct_rows(route, near, far):
    return pl.pallas_call(
        direct_body,
        out_shape=jax.ShapeDtypeStruct((PAIR_DEV,) + near[0].shape[1:], BF16),
        in_specs=[SMEM] + [ANY] * (2 * len(near)),
        out_specs=VMEM,
        scratch_shapes=[pltpu.SemaphoreType.DMA((PAIR_DEV,))],
    )(route, *near, *far)


def turn_body(route, info, *rest, rows_split):
    blocks, outs = rest[:-(rows_split + 3)], rest[-(rows_split + 3):-3]
    held, turned, sem = rest[-3:]
    half = len(blocks) // 2
    fetch(route, blocks[:half], blocks[half:], held, sem, range(PAIR_DEV, 2 * PAIR_DEV))
    row = info[0, ROW]
    width = turned.shape[2]
    for t in range(PAIR_DEV):
        x = held[t].astype(F32).T
        for s in range(rows_split):
            turned[t, s] = x[s * width:(s + 1) * width]
    for s in range(rows_split):
        for t in range(PAIR_DEV):
            outs[s][t] = turned[t, row ^ s].astype(BF16)


def turn(route, info, near, far, rows_split):
    rows, columns = near[0].shape[1:]
    width = columns // rows_split
    return pl.pallas_call(
        functools.partial(turn_body, rows_split=rows_split),
        out_shape=[jax.ShapeDtypeStruct((PAIR_DEV, width, rows), BF16)] * rows_split,
        in_specs=[SMEM, SMEM] + [ANY] * (2 * len(near)),
        out_specs=[VMEM] * rows_split,
        scratch_shapes=[
            pltpu.VMEM((PAIR_DEV, rows, columns), BF16),
            pltpu.VMEM((PAIR_DEV, rows_split, width, rows), F32),
            pltpu.SemaphoreType.DMA((PAIR_DEV,)),
        ],
    )(route, info, *near, *far)


def join_body(info, *rest, rows_split):
    pieces, mirror, placed = rest[:rows_split], rest[rows_split], rest[rows_split + 1]
    row = info[0, ROW]
    for s in range(rows_split):
        for t in range(PAIR_DEV):
            placed[t, row ^ s] = pieces[s][t].astype(F32)
    whole = [jnp.concatenate([placed[t, s] for s in range(rows_split)], axis=1) for t in range(PAIR_DEV)]
    mirror[...] = jnp.stack(whole, axis=1).astype(BF16)


def join(info, pieces):
    rows_split = len(pieces)
    _, height, width = pieces[0].shape
    return pl.pallas_call(
        functools.partial(join_body, rows_split=rows_split),
        out_shape=jax.ShapeDtypeStruct((height, PAIR_DEV, width * rows_split), BF16),
        in_specs=[SMEM] + [VMEM] * rows_split,
        out_specs=VMEM,
        scratch_shapes=[pltpu.VMEM((PAIR_DEV, rows_split, height, width), F32)],
    )(info, *pieces)


def shards(valence_bands, conduction_bands, screened, pair_list, transfer_index, owner_map):
    groups = lax.axis_size("pb")
    rows_split = lax.axis_size("row")
    total = pair_list.shape[0]
    slots = -(-min(2 * MOST, total - (groups - 2)) // 2)
    nc, nv = conduction_bands.shape[1], valence_bands.shape[1]
    per = nv // rows_split

    def away(x, k):
        return lax.ppermute(x, "pb", [(i, i ^ k) for i in range(groups)])

    def along(x, k):
        return lax.ppermute(x, "row", [(i, i ^ k) for i in range(rows_split)])

    w_own = screened[0]
    w_other = away(w_own, 1)
    bands = jnp.concatenate([conduction_bands[0], valence_bands[0]], axis=0)
    con = []
    for s in range(1, rows_split):
        con.append(along(conduction_bands[0], s))
    info, route = tables(pair_list, transfer_index, owner_map, slots, groups, rows_split)
    own = jnp.stack([bands] + [away(bands, 2 * k) for k in range(1, groups // 2)])
    con_rest = jnp.concatenate(con, axis=0)
    con_rest, info, route = lax.optimization_barrier((con_rest, info, route))
    own_rest = jnp.stack([con_rest] + [away(con_rest, 2 * k) for k in range(1, groups // 2)])
    other = away(own, 1)
    other_rest = away(own_rest, 1)

    before = []

    def some_slots(which, early=None):
        table = info
        if before:
            table, _ = lax.optimization_barrier((info, before[-1]))
        pieces = pair_call(table, which, own, own_rest, other, other_rest, w_own, w_other, rows_split)
        before.append(pieces[0])
        shares = [pieces[0]]
        for s in range(1, rows_split):
            shares.append(along(pieces[s], s))
        if early is not None:
            shares, early[:] = lax.optimization_barrier((shares, list(early)))
        return functools.reduce(lambda a, b: a + b, [x.astype(F32) for x in shares]).astype(BF16)

    def spread(summed, count):
        x = summed.reshape(per, nv, count, nc, nc).transpose(2, 0, 3, 1, 4).reshape(count, per * nc, nv * nc)
        out = [x]
        for k in range(1, groups // 2):
            out.append(away(x, 2 * k))
        return out + [away(x, 1) for x in out]

    def group_of(s, early=None):
        which = tuple(range(s, min(s + GROUP, slots)))
        return spread(some_slots(which, early), len(which))

    usual = min(slots, 2 * GROUP)
    more = []
    if slots > usual:
        shape = (per * nc, nv * nc)

        def deep():
            before.clear()
            more = [group_of(s) for s in range(usual, slots, GROUP)]
            return [x for m in more for x in m]

        def flat():
            counts = [min(GROUP, slots - s) for s in range(usual, slots, GROUP)]
            return [jnp.zeros((count,) + shape, BF16) for count in counts for _ in range(groups)]

        more = list(lax.cond(info[0, DEEP] > usual, deep, flat))
    before.clear()
    starts = list(range(0, usual, GROUP))
    held = [group_of(s, more if s == starts[-1] and more else None) for s in starts]
    held += [more[i:i + groups] for i in range(0, len(more), groups)]
    near = [h[x] for x in range(groups // 2) for h in held]
    far = [h[x] for x in range(groups // 2, groups) for h in held]
    pieces = turn(route, info, near, far, rows_split)
    direct = direct_rows(route, near, far)
    got = [pieces[0]] + [along(pieces[s], s) for s in range(1, rows_split)]
    return direct, join(info, got).transpose(1, 0, 2)


def rank_table(labels, groups, slots_per):
    total_rows = labels.shape[0]
    member = (labels[None, :] == jnp.arange(groups, dtype=jnp.int32)[:, None]).astype(jnp.int32)
    before = jnp.cumsum(member, axis=1) - 1
    placed = member[:, None, :] * (
        before[:, None, :] == jnp.arange(slots_per, dtype=jnp.int32)[None, :, None]
    ).astype(jnp.int32)
    numbers = jnp.arange(total_rows, dtype=jnp.int32) + 1
    return jnp.sum(placed * numbers[None, None, :], axis=2) - 1


def whole_pair(val_first, val_second, con_first, con_second, screen_rows):
    val_count = val_first.shape[0]
    con_count = con_first.shape[0]
    val_pairs = val_first[:, None, :].astype(jnp.float32) * val_second[None, :, :].astype(
        jnp.float32
    )
    val_pairs = val_pairs.reshape(val_count * val_count, val_first.shape[1]).astype(jnp.bfloat16)
    con_pairs = con_first[:, None, :].astype(jnp.float32) * con_second[None, :, :].astype(
        jnp.float32
    )
    con_pairs = con_pairs.reshape(con_count * con_count, con_first.shape[1]).astype(jnp.bfloat16)
    interim = lax.dot_general(
        screen_rows, con_pairs, (((1,), (1,)), ((), ())), preferred_element_type=jnp.float32
    ).astype(jnp.bfloat16)
    partial_sum = jnp.dot(val_pairs, interim, preferred_element_type=jnp.float32)
    partial_sum = partial_sum.reshape(val_count, val_count, con_count, con_count).transpose(
        0, 2, 1, 3
    )
    return partial_sum.reshape(val_count * con_count, val_count * con_count)


def plain_shards(valence_bands, conduction_bands, screened, pair_list, transfer_index, owner_map):
    groups = lax.axis_size("pb")
    rows_split = lax.axis_size("row")
    device = lax.axis_index("pb")
    val_all, con_local = (
        lax.all_gather(valence_bands, "pb", axis=0, tiled=True),
        lax.all_gather(conduction_bands, "pb", axis=0, tiled=True),
    )
    slot_table = rank_table(transfer_index[:, 0], groups, MOST)
    own_slots = lax.dynamic_index_in_dim(slot_table, device, 0, keepdims=False)
    live_pair = jnp.maximum(own_slots, 0)
    slot_first = jnp.take(owner_map, jnp.take(pair_list[:, 0], live_pair))
    slot_second = jnp.take(owner_map, jnp.take(pair_list[:, 1], live_pair))
    val_first = jnp.take(val_all, slot_first, axis=0)
    val_second = jnp.take(val_all, slot_second, axis=0)
    con_full = lax.all_gather(con_local, "row", axis=2, tiled=True)
    con_first = jnp.take(con_full, slot_first, axis=0)
    con_second = jnp.take(con_full, slot_second, axis=0)
    screen_rows = screened[0]

    def one_slot(operands):
        return whole_pair(operands[0], operands[1], operands[2], operands[3], screen_rows)

    partials = lax.map(one_slot, (val_first, val_second, con_first, con_second))
    shares = lax.psum_scatter(partials, "row", scatter_dimension=1, tiled=True).astype(jnp.bfloat16)
    band_rows = shares.shape[1]
    mirror_table = rank_table(jnp.take(owner_map, pair_list[:, 1]), groups, PAIR_DEV)
    flat_slots = slot_table.reshape(-1)
    own_direct = device * PAIR_DEV + jnp.arange(PAIR_DEV, dtype=jnp.int32)
    own_mirror = lax.dynamic_index_in_dim(mirror_table, device, 0, keepdims=False)
    wanted = jnp.concatenate([own_direct, own_mirror])
    select = (wanted[:, None] == flat_slots[None, :]).astype(jnp.bfloat16)
    arrived = jnp.einsum(
        "ji,ixy->jxy",
        select,
        lax.all_gather(shares, "pb", axis=0, tiled=True),
        preferred_element_type=jnp.float32,
    )
    direct = arrived[:PAIR_DEV].astype(jnp.bfloat16)
    mirror_rows = arrived[PAIR_DEV:].astype(jnp.bfloat16)
    turned = jnp.transpose(mirror_rows, (0, 2, 1)).reshape(
        PAIR_DEV, rows_split, band_rows, band_rows
    )
    swapped = lax.all_to_all(turned, "row", split_axis=1, concat_axis=3, tiled=True)
    mirror = swapped.reshape(PAIR_DEV, band_rows, band_rows * rows_split)
    return (direct, mirror)


def solution(mesh):
    in_specs = (P("pb", None, "row"), P("pb", None, "row"), P("pb", "row", None), P(), P(), P())
    out_specs = (P("pb", "row", None), P("pb", "row", None))

    def step(valence_bands, conduction_bands, *rest):
        groups, rows_split = mesh.shape["pb"], mesh.shape["row"]
        nv, nc = valence_bands.shape[1], conduction_bands.shape[1]
        even = nv == nc and nv % rows_split == 0 and groups & (groups - 1) == 0 and rows_split & (rows_split - 1) == 0 and groups >= 4
        body = shards if even else plain_shards

        mapped = jax.shard_map(body, mesh=mesh, in_specs=in_specs, out_specs=out_specs, check_vma=False)
        return mapped(valence_bands, conduction_bands, *rest)

    return step
```

profile of v0, /device:TPU:0, one launch (start us, length us, event | category | flops | bytes accessed | tf_op | source)
XLA Modules:
  0.0 125.3 jit_solution(9391922442501987286)
XLA Ops:
  1.2 2.6 %collective-permute-start.10 = (bf16[20,1024]{1,0:T(8,128)(2,1)}, bf16[20,1024]{1,0:T(8,128)(2,1)S(1)}, u32[]{:S(2)}, u32[]{:S(2)}) collective-permute-start(bf16[20,1024]{1,0:T(8,128)(2,1)} %bitcast.30), channel_id=1, source_target_pairs={{0,1},{1,0},{2,3},{3,2},{4,5},{5,4},{6,7},{7,6},{8,9},{9,8},{10,11... | collective-permute-start | bytes 122888 | tf_op jit(solution)/shard_map/ppermute | solution.py:350
  3.9 2.6 %collective-permute-start.11 = (bf16[20,1024]{1,0:T(8,128)(2,1)}, bf16[20,1024]{1,0:T(8,128)(2,1)S(1)}, u32[]{:S(2)}, u32[]{:S(2)}) collective-permute-start(bf16[20,1024]{1,0:T(8,128)(2,1)} %bitcast.31), channel_id=1, source_target_pairs={{0,2},{1,3},{2,0},{3,1},{4,6},{5,7},{6,4},{7,5},{8,10},{9,11},{10,... | collective-permute-start | bytes 122888 | tf_op jit(solution)/shard_map/ppermute | solution.py:350
  6.4 2.3 %shard_map.77 = (s32[5,8]{1,0:T(8,128)S(1)}, s32[2,4,2]{2,1,0:T(4,128)}) custom-call(s32[2,16]{1,0:T(2,128)} %bitcast.41, s32[16]{0:T(128)} %bitcast.42, s32[8]{0:T(128)} %owners.1), custom_call_target="tpu_custom_call" | custom-call | tf_op jit(solution)/shard_map/pallas_call | solution.py:92
  8.7 1.4 %collective-permute-done.11 = bf16[20,1024]{1,0:T(8,128)(2,1)S(1)} collective-permute-done((bf16[20,1024]{1,0:T(8,128)(2,1)}, bf16[20,1024]{1,0:T(8,128)(2,1)S(1)}, u32[]{:S(2)}, u32[]{:S(2)}) %collective-permute-start.11) | collective-permute-done | bytes 40992 | tf_op jit(solution)/shard_map/ppermute | solution.py:350
  10.2 2.4 %collective-permute-done.12 = bf16[20,1024]{1,0:T(8,128)(2,1)S(1)} collective-permute-done((bf16[20,1024]{1,0:T(8,128)(2,1)}, bf16[20,1024]{1,0:T(8,128)(2,1)S(1)}, u32[]{:S(2)}, u32[]{:S(2)}) %collective-permute-start.12) | collective-permute-done | bytes 40992 | tf_op jit(solution)/shard_map/ppermute | solution.py:350
  12.6 1.6 %collective-permute-start.16 = (bf16[60,1024]{1,0:T(8,128)(2,1)S(1)}, bf16[60,1024]{1,0:T(8,128)(2,1)S(1)}, u32[]{:S(2)}, u32[]{:S(2)}) collective-permute-start(bf16[60,1024]{1,0:T(8,128)(2,1)S(1)} %pad_maximum_fusion.2), channel_id=1, source_target_pairs={{0,8},{4,12},{8,0},{12,4},{16,24},{20,28},{24,16},{28,20},{1,9},{5... | collective-permute-start | bytes 368648 | tf_op jit(solution)/shard_map/ppermute | solution.py:347
  14.1 1.5 %collective-permute-start.17 = (bf16[60,1024]{1,0:T(8,128)(2,1)S(1)}, bf16[60,1024]{1,0:T(8,128)(2,1)S(1)}, u32[]{:S(2)}, u32[]{:S(2)}) collective-permute-start(bf16[60,1024]{1,0:T(8,128)(2,1)S(1)} %pad_maximum_fusion.2), channel_id=1, source_target_pairs={{0,16},{4,20},{8,24},{12,28},{16,0},{20,4},{24,8},{28,12},{1,17},{... | collective-permute-start | bytes 368648 | tf_op jit(solution)/shard_map/ppermute | solution.py:347
  17.0 1.6 %collective-permute-start.13 = (bf16[40,1024]{1,0:T(8,128)(2,1)S(1)}, bf16[40,1024]{1,0:T(8,128)(2,1)S(1)}, u32[]{:S(2)}, u32[]{:S(2)}) collective-permute-start(bf16[40,1024]{1,0:T(8,128)(2,1)S(1)} %pad_maximum_fusion.3), channel_id=1, source_target_pairs={{0,8},{4,12},{8,0},{12,4},{16,24},{20,28},{24,16},{28,20},{1,9},{5... | collective-permute-start | bytes 245768 | tf_op jit(solution)/shard_map/ppermute | solution.py:347
  18.9 1.5 %collective-permute-start.14 = (bf16[40,1024]{1,0:T(8,128)(2,1)S(1)}, bf16[40,1024]{1,0:T(8,128)(2,1)S(1)}, u32[]{:S(2)}, u32[]{:S(2)}) collective-permute-start(bf16[40,1024]{1,0:T(8,128)(2,1)S(1)} %pad_maximum_fusion.3), channel_id=1, source_target_pairs={{0,16},{4,20},{8,24},{12,28},{16,0},{20,4},{24,8},{28,12},{1,17},{... | collective-permute-start | bytes 245768 | tf_op jit(solution)/shard_map/ppermute | solution.py:347
  20.4 3.1 %collective-permute-done.17 = bf16[60,1024]{1,0:T(8,128)(2,1)S(1)} collective-permute-done((bf16[60,1024]{1,0:T(8,128)(2,1)S(1)}, bf16[60,1024]{1,0:T(8,128)(2,1)S(1)}, u32[]{:S(2)}, u32[]{:S(2)}) %collective-permute-start.17) | collective-permute-done | bytes 122912 | tf_op jit(solution)/shard_map/ppermute | solution.py:347
  24.3 4.5 %collective-permute-done.15 = bf16[40,1024]{1,0:T(8,128)(2,1)S(1)} collective-permute-done((bf16[40,1024]{1,0:T(8,128)(2,1)S(1)}, bf16[40,1024]{1,0:T(8,128)(2,1)S(1)}, u32[]{:S(2)}, u32[]{:S(2)}) %collective-permute-start.15) | collective-permute-done | bytes 81952 | tf_op jit(solution)/shard_map/ppermute | solution.py:347
  30.6 13.7 %shard_map.78 = (bf16[100,800]{1,0:T(8,128)(2,1)}, bf16[100,800]{1,0:T(8,128)(2,1)}, bf16[100,800]{1,0:T(8,128)(2,1)}, bf16[100,800]{1,0:T(8,128)(2,1)}) custom-call(s32[5,8]{1,0:T(8,128)S(1)} %get-tuple-element.74.info, bf16[4,40,1024]{2,1,0:T(8,128)(2,1)S(1)} %pad_maximum_fusion.1.own, bf16[4,60,1024]{2,1,0:T(8,128)(2,1)S(1)} %pad_maximum_fusion.own_rest, ...), custom_call_target="tpu_custom_call" | custom-call | flops 6710886400 | bytes 8388608 | tf_op jit(solution)/shard_map/pallas_call | solution.py:231
  44.3 1.7 %shard_map.79 = (bf16[100,800]{1,0:T(8,128)(2,1)}, bf16[100,800]{1,0:T(8,128)(2,1)}, bf16[100,800]{1,0:T(8,128)(2,1)}, bf16[100,800]{1,0:T(8,128)(2,1)}) custom-call(s32[5,8]{1,0:T(8,128)S(1)} %get-tuple-element.74.info, bf16[4,40,1024]{2,1,0:T(8,128)(2,1)S(1)} %pad_maximum_fusion.1.own, bf16[4,60,1024]{2,1,0:T(8,128)(2,1)S(1)} %pad_maximum_fusion.own_rest, ...), custom_call_target="tpu_custom_call" | custom-call | flops 6710886400 | bytes 8388608 | tf_op jit(solution)/shard_map/pallas_call | solution.py:231
  46.1 5.2 %conditional.1 = (bf16[1,100,400]{2,1,0:T(8,128)(2,1)}, bf16[1,100,400]{2,1,0:T(8,128)(2,1)}, bf16[1,100,400]{2,1,0:T(8,128)(2,1)}, bf16[1,100,400]{2,1,0:T(8,12...) conditional(s32[]{:T(128)} %bitcast.15, () %tuple.21, ...), branch_computations={%region_0.0_spmd, %region_1.0_spmd} | conditional | flops 3355763200 | bytes 12469072 | solution.py:406
  51.4 1.7 %collective-permute-start.26 = (bf16[100,800]{1,0:T(8,128)(2,1)S(1)}, bf16[100,800]{1,0:T(8,128)(2,1)S(1)}, u32[]{:S(2)}, u32[]{:S(2)}) collective-permute-start(bf16[100,800]{1,0:T(8,128)(2,1)S(1)} %copy-done.24), channel_id=1, source_target_pairs={{0,2},{1,3},{2,0},{3,1},{4,6},{5,7},{6,4},{7,5},{8,10},{9,11},{10,... | collective-permute-start | bytes 480008 | tf_op jit(solution)/shard_map/ppermute | solution.py:350
  53.1 2.6 %collective-permute-start.27 = (bf16[100,800]{1,0:T(8,128)(2,1)S(1)}, bf16[100,800]{1,0:T(8,128)(2,1)S(1)}, u32[]{:S(2)}, u32[]{:S(2)}) collective-permute-start(bf16[100,800]{1,0:T(8,128)(2,1)S(1)} %copy-done.23), channel_id=1, source_target_pairs={{0,3},{1,2},{2,1},{3,0},{4,7},{5,6},{6,5},{7,4},{8,11},{9,10},{10,... | collective-permute-start | bytes 480008 | tf_op jit(solution)/shard_map/ppermute | solution.py:350
  55.7 1.8 %collective-permute-start.23 = (bf16[100,800]{1,0:T(8,128)(2,1)}, bf16[100,800]{1,0:T(8,128)(2,1)}, u32[]{:S(2)}, u32[]{:S(2)}) collective-permute-start(bf16[100,800]{1,0:T(8,128)(2,1)} %get-tuple-element.72), channel_id=1, source_target_pairs={{0,2},{1,3},{2,0},{3,1},{4,6},{5,7},{6,4},{7,5},{8,10},{9,11},{10,... | collective-permute-start | bytes 480008 | tf_op jit(solution)/shard_map/ppermute | solution.py:350
  57.5 2.6 %collective-permute-start.24 = (bf16[100,800]{1,0:T(8,128)(2,1)}, bf16[100,800]{1,0:T(8,128)(2,1)}, u32[]{:S(2)}, u32[]{:S(2)}) collective-permute-start(bf16[100,800]{1,0:T(8,128)(2,1)} %get-tuple-element.73), channel_id=1, source_target_pairs={{0,3},{1,2},{2,1},{3,0},{4,7},{5,6},{6,5},{7,4},{8,11},{9,10},{10,... | collective-permute-start | bytes 480008 | tf_op jit(solution)/shard_map/ppermute | solution.py:350
  60.1 8.3 %collective-permute-done.26 = bf16[100,800]{1,0:T(8,128)(2,1)S(1)} collective-permute-done((bf16[100,800]{1,0:T(8,128)(2,1)S(1)}, bf16[100,800]{1,0:T(8,128)(2,1)S(1)}, u32[]{:S(2)}, u32[]{:S(2)}) %collective-permute-start.26) | collective-permute-done | bytes 160032 | tf_op jit(solution)/shard_map/ppermute | solution.py:350
  68.5 1.3 %reshape.32 = bf16[5,20,2,20,20]{4,3,2,1,0:T(8,128)(2,1)S(1)} reshape(bf16[100,800]{1,0:T(8,128)(2,1)S(1)} %add_convert_fusion.1) | data formatting | bytes 320000 | tf_op jit(solution)/shard_map/reshape | solution.py:382
  70.9 12.6 %collective-permute-start.31 = (bf16[2,100,400]{2,1,0:T(8,128)(2,1)S(1)}, bf16[2,100,400]{2,1,0:T(8,128)(2,1)S(1)}, u32[]{:S(2)}, u32[]{:S(2)}) collective-permute-start(bf16[2,100,400]{2,1,0:T(8,128)(2,1)S(1)} %reshape.33.rest_1_), channel_id=1, source_target_pairs={{0,16},{4,20},{8,24},{12,28},{16,0},{20,4},{24,8},{28,12},{1,17},{... | collective-permute-start | bytes 480008 | tf_op jit(solution)/shard_map/ppermute | solution.py:347
  83.5 1.1 add_convert_fusion.2
  84.6 1.3 %reshape.30 = bf16[5,20,2,20,20]{4,3,2,1,0:T(8,128)(2,1)S(1)} reshape(bf16[100,800]{1,0:T(8,128)(2,1)S(1)} %add_convert_fusion.2) | data formatting | bytes 320000 | tf_op jit(solution)/shard_map/reshape | solution.py:382
  87.0 1.4 %collective-permute-start.28 = (bf16[2,100,400]{2,1,0:T(8,128)(2,1)S(1)}, bf16[2,100,400]{2,1,0:T(8,128)(2,1)S(1)}, u32[]{:S(2)}, u32[]{:S(2)}) collective-permute-start(bf16[2,100,400]{2,1,0:T(8,128)(2,1)S(1)} %reshape.31.rest_0_), channel_id=1, source_target_pairs={{0,8},{4,12},{8,0},{12,4},{16,24},{20,28},{24,16},{28,20},{1,9},{5... | collective-permute-start | bytes 480008 | tf_op jit(solution)/shard_map/ppermute | solution.py:347
  88.4 7.7 %collective-permute-start.30 = (bf16[2,100,400]{2,1,0:T(8,128)(2,1)S(1)}, bf16[2,100,400]{2,1,0:T(8,128)(2,1)S(1)}, u32[]{:S(2)}, u32[]{:S(2)}) collective-permute-start(bf16[2,100,400]{2,1,0:T(8,128)(2,1)S(1)} %reshape.31.rest_0_), channel_id=1, source_target_pairs={{0,16},{4,20},{8,24},{12,28},{16,0},{20,4},{24,8},{28,12},{1,17},{... | collective-permute-start | bytes 480008 | tf_op jit(solution)/shard_map/ppermute | solution.py:347
  96.8 9.5 %collective-permute-done.30.rest_6_ = bf16[2,100,400]{2,1,0:T(8,128)(2,1)S(1)} collective-permute-done((bf16[2,100,400]{2,1,0:T(8,128)(2,1)S(1)}, bf16[2,100,400]{2,1,0:T(8,128)(2,1)S(1)}, u32[]{:S(2)}, u32[]{:S(2)}) %collective-permute-start.30) | collective-permute-done | bytes 160032 | tf_op jit(solution)/shard_map/ppermute | solution.py:347
  109.7 2.5 %shard_map.81 = (bf16[2,100,100]{2,1,0:T(8,128)(2,1)}, bf16[2,100,100]{2,1,0:T(8,128)(2,1)}, bf16[2,100,100]{2,1,0:T(8,128)(2,1)}, bf16[2,100,100]{2,1,0:T(8,128)(2,1)}) custom-call(s32[2,4,2]{2,1,0:T(4,128)} %get-tuple-element.67.route, s32[5,8]{1,0:T(8,128)S(1)} %get-tuple-element.74.info, bf16[2,100,400]{2,1,0:T(8,128)(2,1)} %copy-done.1, ...), custom_call_target="tpu_custom_call" | custom-call | tf_op jit(solution)/shard_map/pallas_call | solution.py:303
  112.3 2.9 %collective-permute-start.42 = (bf16[2,100,100]{2,1,0:T(8,128)(2,1)}, bf16[2,100,100]{2,1,0:T(8,128)(2,1)S(1)}, u32[]{:S(2)}, u32[]{:S(2)}) collective-permute-start(bf16[2,100,100]{2,1,0:T(8,128)(2,1)} %get-tuple-element.100), channel_id=1, source_target_pairs={{0,1},{1,0},{2,3},{3,2},{4,5},{5,4},{6,7},{7,6},{8,9},{9,8},{10,11... | collective-permute-start | bytes 120008 | tf_op jit(solution)/shard_map/ppermute | solution.py:350
  115.6 2.0 %collective-permute-start.44 = (bf16[2,100,100]{2,1,0:T(8,128)(2,1)}, bf16[2,100,100]{2,1,0:T(8,128)(2,1)S(1)}, u32[]{:S(2)}, u32[]{:S(2)}) collective-permute-start(bf16[2,100,100]{2,1,0:T(8,128)(2,1)} %get-tuple-element.102), channel_id=1, source_target_pairs={{0,3},{1,2},{2,1},{3,0},{4,7},{5,6},{6,5},{7,4},{8,11},{9,10},{10,... | collective-permute-start | bytes 120008 | tf_op jit(solution)/shard_map/ppermute | solution.py:350
  117.6 2.4 %shard_map.80 = bf16[2,100,400]{2,1,0:T(8,128)(2,1)} custom-call(s32[2,4,2]{2,1,0:T(4,128)} %get-tuple-element.67.route, bf16[2,100,400]{2,1,0:T(8,128)(2,1)} %copy-done.1, bf16[2,100,400]{2,1,0:T(8,128)(2,1)} %copy-done, bf16[1,100,400]{2,1,0:T(8,128)(2,1)} %get-tuple-element.91.rest_2_, bf16[2,100,400]{2,1,0:T(8,128)(2,1)} %copy-done.5, ...), custom_call_target="tpu_custom_call" | custom-call | tf_op jit(solution)/shard_map/pallas_call | solution.py:275
  120.1 1.8 %copy.15 = bf16[2,100,400]{2,0,1:T(2,128)(2,1)} copy(bf16[2,100,400]{2,1,0:T(8,128)(2,1)} %shard_map.80) | data formatting | bytes 320000
  123.3 2.0 %shard_map.82 = bf16[100,2,400]{2,1,0:T(2,128)(2,1)} custom-call(s32[5,8]{1,0:T(8,128)S(1)} %get-tuple-element.74.info, bf16[2,100,100]{2,1,0:T(8,128)(2,1)} %get-tuple-element.99.rest_0_, bf16[2,100,100]{2,1,0:T(8,128)(2,1)} %copy-done.19, bf16[2,100,100]{2,1,0:T(8,128)(2,1)} %copy-done.20, bf16[2,100,100]{2,1,0:T(8,128)(2,1)} %copy-done.21), custom_call_target="tpu_custom_call" | custom-call | tf_op jit(solution)/shard_map/pallas_call | solution.py:329
  (118 shorter events, 17.6 us)
Async XLA Ops:
  0.7 29.9 %collective-permute-start.21 = (bf16[1024,4096]{1,0:T(8,128)(2,1)}, bf16[1024,4096]{1,0:T(8,128)(2,1)}, u32[]{:S(2)}, u32[]{:S(2)}) collective-permute-start(bf16[1024,4096]{1,0:T(8,128)(2,1)} %bitcast.19), channel_id=1, source_target_pairs={{0,4},{4,0},{8,12},{12,8},{16,20},{20,16},{24,28},{28,24},{1,5},{5... | collective-permute-start | bytes 25165832 | tf_op jit(solution)/shard_map/ppermute | solution.py:347
  1.2 7.5 %collective-permute-start.10 = (bf16[20,1024]{1,0:T(8,128)(2,1)}, bf16[20,1024]{1,0:T(8,128)(2,1)S(1)}, u32[]{:S(2)}, u32[]{:S(2)}) collective-permute-start(bf16[20,1024]{1,0:T(8,128)(2,1)} %bitcast.30), channel_id=1, source_target_pairs={{0,1},{1,0},{2,3},{3,2},{4,5},{5,4},{6,7},{7,6},{8,9},{9,8},{10,11... | collective-permute-start | bytes 122888 | tf_op jit(solution)/shard_map/ppermute | solution.py:350
  3.9 6.3 %collective-permute-start.11 = (bf16[20,1024]{1,0:T(8,128)(2,1)}, bf16[20,1024]{1,0:T(8,128)(2,1)S(1)}, u32[]{:S(2)}, u32[]{:S(2)}) collective-permute-start(bf16[20,1024]{1,0:T(8,128)(2,1)} %bitcast.31), channel_id=1, source_target_pairs={{0,2},{1,3},{2,0},{3,1},{4,6},{5,7},{6,4},{7,5},{8,10},{9,11},{10,... | collective-permute-start | bytes 122888 | tf_op jit(solution)/shard_map/ppermute | solution.py:350
  6.4 6.1 %collective-permute-start.12 = (bf16[20,1024]{1,0:T(8,128)(2,1)}, bf16[20,1024]{1,0:T(8,128)(2,1)S(1)}, u32[]{:S(2)}, u32[]{:S(2)}) collective-permute-start(bf16[20,1024]{1,0:T(8,128)(2,1)} %bitcast.32), channel_id=1, source_target_pairs={{0,3},{1,2},{2,1},{3,0},{4,7},{5,6},{6,5},{7,4},{8,11},{9,10},{10,... | collective-permute-start | bytes 122888 | tf_op jit(solution)/shard_map/ppermute | solution.py:350
  12.6 6.3 %collective-permute-start.16 = (bf16[60,1024]{1,0:T(8,128)(2,1)S(1)}, bf16[60,1024]{1,0:T(8,128)(2,1)S(1)}, u32[]{:S(2)}, u32[]{:S(2)}) collective-permute-start(bf16[60,1024]{1,0:T(8,128)(2,1)S(1)} %pad_maximum_fusion.2), channel_id=1, source_target_pairs={{0,8},{4,12},{8,0},{12,4},{16,24},{20,28},{24,16},{28,20},{1,9},{5... | collective-permute-start | bytes 368648 | tf_op jit(solution)/shard_map/ppermute | solution.py:347
  14.1 9.3 %collective-permute-start.17 = (bf16[60,1024]{1,0:T(8,128)(2,1)S(1)}, bf16[60,1024]{1,0:T(8,128)(2,1)S(1)}, u32[]{:S(2)}, u32[]{:S(2)}) collective-permute-start(bf16[60,1024]{1,0:T(8,128)(2,1)S(1)} %pad_maximum_fusion.2), channel_id=1, source_target_pairs={{0,16},{4,20},{8,24},{12,28},{16,0},{20,4},{24,8},{28,12},{1,17},{... | collective-permute-start | bytes 368648 | tf_op jit(solution)/shard_map/ppermute | solution.py:347
  15.7 7.8 %collective-permute-start.18 = (bf16[60,1024]{1,0:T(8,128)(2,1)S(1)}, bf16[60,1024]{1,0:T(8,128)(2,1)S(1)}, u32[]{:S(2)}, u32[]{:S(2)}) collective-permute-start(bf16[60,1024]{1,0:T(8,128)(2,1)S(1)} %pad_maximum_fusion.2), channel_id=1, source_target_pairs={{0,24},{4,28},{8,16},{12,20},{16,8},{20,12},{24,0},{28,4},{1,25},{... | collective-permute-start | bytes 368648 | tf_op jit(solution)/shard_map/ppermute | solution.py:347
  17.0 6.7 %collective-permute-start.13 = (bf16[40,1024]{1,0:T(8,128)(2,1)S(1)}, bf16[40,1024]{1,0:T(8,128)(2,1)S(1)}, u32[]{:S(2)}, u32[]{:S(2)}) collective-permute-start(bf16[40,1024]{1,0:T(8,128)(2,1)S(1)} %pad_maximum_fusion.3), channel_id=1, source_target_pairs={{0,8},{4,12},{8,0},{12,4},{16,24},{20,28},{24,16},{28,20},{1,9},{5... | collective-permute-start | bytes 245768 | tf_op jit(solution)/shard_map/ppermute | solution.py:347
  18.9 5.5 %collective-permute-start.14 = (bf16[40,1024]{1,0:T(8,128)(2,1)S(1)}, bf16[40,1024]{1,0:T(8,128)(2,1)S(1)}, u32[]{:S(2)}, u32[]{:S(2)}) collective-permute-start(bf16[40,1024]{1,0:T(8,128)(2,1)S(1)} %pad_maximum_fusion.3), channel_id=1, source_target_pairs={{0,16},{4,20},{8,24},{12,28},{16,0},{20,4},{24,8},{28,12},{1,17},{... | collective-permute-start | bytes 245768 | tf_op jit(solution)/shard_map/ppermute | solution.py:347
  23.5 5.3 %collective-permute-start.15 = (bf16[40,1024]{1,0:T(8,128)(2,1)S(1)}, bf16[40,1024]{1,0:T(8,128)(2,1)S(1)}, u32[]{:S(2)}, u32[]{:S(2)}) collective-permute-start(bf16[40,1024]{1,0:T(8,128)(2,1)S(1)} %pad_maximum_fusion.3), channel_id=1, source_target_pairs={{0,24},{4,28},{8,16},{12,20},{16,8},{20,12},{24,0},{28,4},{1,25},{... | collective-permute-start | bytes 245768 | tf_op jit(solution)/shard_map/ppermute | solution.py:347
  23.6 7.0 %collective-permute-start.20 = (bf16[4,60,1024]{2,1,0:T(8,128)(2,1)S(1)}, bf16[4,60,1024]{2,1,0:T(8,128)(2,1)S(1)}, u32[]{:S(2)}, u32[]{:S(2)}) collective-permute-start(bf16[4,60,1024]{2,1,0:T(8,128)(2,1)S(1)} %pad_maximum_fusion.own_rest), channel_id=1, source_target_pairs={{0,4},{4,0},{8,12},{12,8},{16,20},{20,16},{24,28},{28,24},{1,5},{5... | collective-permute-start | bytes 1474568 | tf_op jit(solution)/shard_map/ppermute | solution.py:347
  46.0 11.5 %collective-permute-start.25 = (bf16[100,800]{1,0:T(8,128)(2,1)}, bf16[100,800]{1,0:T(8,128)(2,1)S(1)}, u32[]{:S(2)}, u32[]{:S(2)}) collective-permute-start(bf16[100,800]{1,0:T(8,128)(2,1)} %get-tuple-element.76), channel_id=1, source_target_pairs={{0,1},{1,0},{2,3},{3,2},{4,5},{5,4},{6,7},{7,6},{8,9},{9,8},{10,11... | collective-permute-start | bytes 480008 | tf_op jit(solution)/shard_map/ppermute | solution.py:350
  51.4 17.0 %collective-permute-start.26 = (bf16[100,800]{1,0:T(8,128)(2,1)S(1)}, bf16[100,800]{1,0:T(8,128)(2,1)S(1)}, u32[]{:S(2)}, u32[]{:S(2)}) collective-permute-start(bf16[100,800]{1,0:T(8,128)(2,1)S(1)} %copy-done.24), channel_id=1, source_target_pairs={{0,2},{1,3},{2,0},{3,1},{4,6},{5,7},{6,4},{7,5},{8,10},{9,11},{10,... | collective-permute-start | bytes 480008 | tf_op jit(solution)/shard_map/ppermute | solution.py:350
  53.1 15.3 %collective-permute-start.27 = (bf16[100,800]{1,0:T(8,128)(2,1)S(1)}, bf16[100,800]{1,0:T(8,128)(2,1)S(1)}, u32[]{:S(2)}, u32[]{:S(2)}) collective-permute-start(bf16[100,800]{1,0:T(8,128)(2,1)S(1)} %copy-done.23), channel_id=1, source_target_pairs={{0,3},{1,2},{2,1},{3,0},{4,7},{5,6},{6,5},{7,4},{8,11},{9,10},{10,... | collective-permute-start | bytes 480008 | tf_op jit(solution)/shard_map/ppermute | solution.py:350
  55.7 27.7 %collective-permute-start.22 = (bf16[100,800]{1,0:T(8,128)(2,1)S(1)}, bf16[100,800]{1,0:T(8,128)(2,1)S(1)}, u32[]{:S(2)}, u32[]{:S(2)}) collective-permute-start(bf16[100,800]{1,0:T(8,128)(2,1)S(1)} %copy-done.22), channel_id=1, source_target_pairs={{0,1},{1,0},{2,3},{3,2},{4,5},{5,4},{6,7},{7,6},{8,9},{9,8},{10,11... | collective-permute-start | bytes 480008 | tf_op jit(solution)/shard_map/ppermute | solution.py:350
  55.7 27.7 %collective-permute-start.23 = (bf16[100,800]{1,0:T(8,128)(2,1)}, bf16[100,800]{1,0:T(8,128)(2,1)}, u32[]{:S(2)}, u32[]{:S(2)}) collective-permute-start(bf16[100,800]{1,0:T(8,128)(2,1)} %get-tuple-element.72), channel_id=1, source_target_pairs={{0,2},{1,3},{2,0},{3,1},{4,6},{5,7},{6,4},{7,5},{8,10},{9,11},{10,... | collective-permute-start | bytes 480008 | tf_op jit(solution)/shard_map/ppermute | solution.py:350
  57.5 26.0 %collective-permute-start.24 = (bf16[100,800]{1,0:T(8,128)(2,1)}, bf16[100,800]{1,0:T(8,128)(2,1)}, u32[]{:S(2)}, u32[]{:S(2)}) collective-permute-start(bf16[100,800]{1,0:T(8,128)(2,1)} %get-tuple-element.73), channel_id=1, source_target_pairs={{0,3},{1,2},{2,1},{3,0},{4,7},{5,6},{6,5},{7,4},{8,11},{9,10},{10,... | collective-permute-start | bytes 480008 | tf_op jit(solution)/shard_map/ppermute | solution.py:350
  70.8 17.6 %collective-permute-start.29 = (bf16[2,100,400]{2,1,0:T(8,128)(2,1)S(1)}, bf16[2,100,400]{2,1,0:T(8,128)(2,1)S(1)}, u32[]{:S(2)}, u32[]{:S(2)}) collective-permute-start(bf16[2,100,400]{2,1,0:T(8,128)(2,1)S(1)} %reshape.33.rest_1_), channel_id=1, source_target_pairs={{0,8},{4,12},{8,0},{12,4},{16,24},{20,28},{24,16},{28,20},{1,9},{5... | collective-permute-start | bytes 480008 | tf_op jit(solution)/shard_map/ppermute | solution.py:347
  70.9 25.3 %collective-permute-start.31 = (bf16[2,100,400]{2,1,0:T(8,128)(2,1)S(1)}, bf16[2,100,400]{2,1,0:T(8,128)(2,1)S(1)}, u32[]{:S(2)}, u32[]{:S(2)}) collective-permute-start(bf16[2,100,400]{2,1,0:T(8,128)(2,1)S(1)} %reshape.33.rest_1_), channel_id=1, source_target_pairs={{0,16},{4,20},{8,24},{12,28},{16,0},{20,4},{24,8},{28,12},{1,17},{... | collective-permute-start | bytes 480008 | tf_op jit(solution)/shard_map/ppermute | solution.py:347
  83.4 12.7 %collective-permute-start.33 = (bf16[2,100,400]{2,1,0:T(8,128)(2,1)S(1)}, bf16[2,100,400]{2,1,0:T(8,128)(2,1)S(1)}, u32[]{:S(2)}, u32[]{:S(2)}) collective-permute-start(bf16[2,100,400]{2,1,0:T(8,128)(2,1)S(1)} %reshape.33.rest_1_), channel_id=1, source_target_pairs={{0,24},{4,28},{8,16},{12,20},{16,8},{20,12},{24,0},{28,4},{1,25},{... | collective-permute-start | bytes 480008 | tf_op jit(solution)/shard_map/ppermute | solution.py:347
  83.4 12.8 %collective-permute-start.35 = (bf16[2,100,400]{2,1,0:T(8,128)(2,1)S(1)}, bf16[2,100,400]{2,1,0:T(8,128)(2,1)}, u32[]{:S(2)}, u32[]{:S(2)}) collective-permute-start(bf16[2,100,400]{2,1,0:T(8,128)(2,1)S(1)} %reshape.33.rest_1_), channel_id=1, source_target_pairs={{0,4},{4,0},{8,12},{12,8},{16,20},{20,16},{24,28},{28,24},{1,5},{5... | collective-permute-start | bytes 480008 | tf_op jit(solution)/shard_map/ppermute | solution.py:347
  87.0 9.8 %collective-permute-start.28 = (bf16[2,100,400]{2,1,0:T(8,128)(2,1)S(1)}, bf16[2,100,400]{2,1,0:T(8,128)(2,1)S(1)}, u32[]{:S(2)}, u32[]{:S(2)}) collective-permute-start(bf16[2,100,400]{2,1,0:T(8,128)(2,1)S(1)} %reshape.31.rest_0_), channel_id=1, source_target_pairs={{0,8},{4,12},{8,0},{12,4},{16,24},{20,28},{24,16},{28,20},{1,9},{5... | collective-permute-start | bytes 480008 | tf_op jit(solution)/shard_map/ppermute | solution.py:347
  88.4 17.9 %collective-permute-start.30 = (bf16[2,100,400]{2,1,0:T(8,128)(2,1)S(1)}, bf16[2,100,400]{2,1,0:T(8,128)(2,1)S(1)}, u32[]{:S(2)}, u32[]{:S(2)}) collective-permute-start(bf16[2,100,400]{2,1,0:T(8,128)(2,1)S(1)} %reshape.31.rest_0_), channel_id=1, source_target_pairs={{0,16},{4,20},{8,24},{12,28},{16,0},{20,4},{24,8},{28,12},{1,17},{... | collective-permute-start | bytes 480008 | tf_op jit(solution)/shard_map/ppermute | solution.py:347
  96.1 10.2 %collective-permute-start.32 = (bf16[2,100,400]{2,1,0:T(8,128)(2,1)S(1)}, bf16[2,100,400]{2,1,0:T(8,128)(2,1)S(1)}, u32[]{:S(2)}, u32[]{:S(2)}) collective-permute-start(bf16[2,100,400]{2,1,0:T(8,128)(2,1)S(1)} %reshape.31.rest_0_), channel_id=1, source_target_pairs={{0,24},{4,28},{8,16},{12,20},{16,8},{20,12},{24,0},{28,4},{1,25},{... | collective-permute-start | bytes 480008 | tf_op jit(solution)/shard_map/ppermute | solution.py:347
  96.1 10.7 %collective-permute-start.34 = (bf16[2,100,400]{2,1,0:T(8,128)(2,1)S(1)}, bf16[2,100,400]{2,1,0:T(8,128)(2,1)S(1)}, u32[]{:S(2)}, u32[]{:S(2)}) collective-permute-start(bf16[2,100,400]{2,1,0:T(8,128)(2,1)S(1)} %reshape.31.rest_0_), channel_id=1, source_target_pairs={{0,4},{4,0},{8,12},{12,8},{16,20},{20,16},{24,28},{28,24},{1,5},{5... | collective-permute-start | bytes 480008 | tf_op jit(solution)/shard_map/ppermute | solution.py:347
  96.2 10.7 %collective-permute-start.37 = (bf16[2,100,400]{2,1,0:T(8,128)(2,1)S(1)}, bf16[2,100,400]{2,1,0:T(8,128)(2,1)S(1)}, u32[]{:S(2)}, u32[]{:S(2)}) collective-permute-start(bf16[2,100,400]{2,1,0:T(8,128)(2,1)S(1)} %collective-permute-done.29.rest_4_), channel_id=1, source_target_pairs={{0,4},{4,0},{8,12},{12,8},{16,20},{20,16},{24,28},{28,24},{1,5},{5... | collective-permute-start | bytes 480008 | tf_op jit(solution)/shard_map/ppermute | solution.py:347
  96.7 10.6 %collective-permute-start.39 = (bf16[2,100,400]{2,1,0:T(8,128)(2,1)S(1)}, bf16[2,100,400]{2,1,0:T(8,128)(2,1)S(1)}, u32[]{:S(2)}, u32[]{:S(2)}) collective-permute-start(bf16[2,100,400]{2,1,0:T(8,128)(2,1)S(1)} %collective-permute-done.31.rest_7_), channel_id=1, source_target_pairs={{0,4},{4,0},{8,12},{12,8},{16,20},{20,16},{24,28},{28,24},{1,5},{5... | collective-permute-start | bytes 480008 | tf_op jit(solution)/shard_map/ppermute | solution.py:347
  106.3 1.8 %collective-permute-start.36 = (bf16[2,100,400]{2,1,0:T(8,128)(2,1)S(1)}, bf16[2,100,400]{2,1,0:T(8,128)(2,1)S(1)}, u32[]{:S(2)}, u32[]{:S(2)}) collective-permute-start(bf16[2,100,400]{2,1,0:T(8,128)(2,1)S(1)} %collective-permute-done.28.rest_3_), channel_id=1, source_target_pairs={{0,4},{4,0},{8,12},{12,8},{16,20},{20,16},{24,28},{28,24},{1,5},{5... | collective-permute-start | bytes 480008 | tf_op jit(solution)/shard_map/ppermute | solution.py:347
  106.9 1.8 %collective-permute-start.40 = (bf16[2,100,400]{2,1,0:T(8,128)(2,1)S(1)}, bf16[2,100,400]{2,1,0:T(8,128)(2,1)S(1)}, u32[]{:S(2)}, u32[]{:S(2)}) collective-permute-start(bf16[2,100,400]{2,1,0:T(8,128)(2,1)S(1)} %collective-permute-done.32.rest_9_), channel_id=1, source_target_pairs={{0,4},{4,0},{8,12},{12,8},{16,20},{20,16},{24,28},{28,24},{1,5},{5... | collective-permute-start | bytes 480008 | tf_op jit(solution)/shard_map/ppermute | solution.py:347
  112.3 9.5 %collective-permute-start.42 = (bf16[2,100,100]{2,1,0:T(8,128)(2,1)}, bf16[2,100,100]{2,1,0:T(8,128)(2,1)S(1)}, u32[]{:S(2)}, u32[]{:S(2)}) collective-permute-start(bf16[2,100,100]{2,1,0:T(8,128)(2,1)} %get-tuple-element.100), channel_id=1, source_target_pairs={{0,1},{1,0},{2,3},{3,2},{4,5},{5,4},{6,7},{7,6},{8,9},{9,8},{10,11... | collective-permute-start | bytes 120008 | tf_op jit(solution)/shard_map/ppermute | solution.py:350
  115.2 7.5 %collective-permute-start.43 = (bf16[2,100,100]{2,1,0:T(8,128)(2,1)}, bf16[2,100,100]{2,1,0:T(8,128)(2,1)S(1)}, u32[]{:S(2)}, u32[]{:S(2)}) collective-permute-start(bf16[2,100,100]{2,1,0:T(8,128)(2,1)} %get-tuple-element.101), channel_id=1, source_target_pairs={{0,2},{1,3},{2,0},{3,1},{4,6},{5,7},{6,4},{7,5},{8,10},{9,11},{10,... | collective-permute-start | bytes 120008 | tf_op jit(solution)/shard_map/ppermute | solution.py:350
  115.6 7.0 %collective-permute-start.44 = (bf16[2,100,100]{2,1,0:T(8,128)(2,1)}, bf16[2,100,100]{2,1,0:T(8,128)(2,1)S(1)}, u32[]{:S(2)}, u32[]{:S(2)}) collective-permute-start(bf16[2,100,100]{2,1,0:T(8,128)(2,1)} %get-tuple-element.102), channel_id=1, source_target_pairs={{0,3},{1,2},{2,1},{3,0},{4,7},{5,6},{6,5},{7,4},{8,11},{9,10},{10,... | collective-permute-start | bytes 120008 | tf_op jit(solution)/shard_map/ppermute | solution.py:350
  (28 other events, 218.1 us)
where the time goes:
time: 126 us; the launch traced here: 125 us
  starting transfers between devices  50.2 us (40%)
  waiting for transfers between devices  32.7 us (26%)
  Pallas kernels  24.7 us (20%)
  local copies, waits for them, and re-layouts  13.7 us (11%)
  other arithmetic  2.22 us (2%)
  between operations  1.74 us (1%)
    ppermute x23, starting transfers between devices, away(): return lax.ppermute(x, 'pb', [(i, i ^ k) for i in range(groups)])  30.9 us
    ppermute x23, waiting for transfers between devices, away(): return lax.ppermute(x, 'pb', [(i, i ^ k) for i in range(groups)])  19.8 us
    ppermute x12, starting transfers between devices, along(): return lax.ppermute(x, 'row', [(i, i ^ k) for i in range(rows_split)])  19.4 us
    pallas_call x2, Pallas kernels, pair_call(): pl.pallas_call(functools.partial(pair_body, slots=slots, rows_split=rows_...  15.4 us
    ppermute x12, waiting for transfers between devices, along(): return lax.ppermute(x, 'row', [(i, i ^ k) for i in range(rows_split)])  12.9 us
    another operation x8, local copies, waits for them, and re-layouts, step(): return mapped(valence_bands, conduction_bands, *rest)  5.2 us
    reshape x4, local copies, waits for them, and re-layouts, spread(): summed.reshape(per, nv, count, nc, nc).transpose(2, 0, 3, 1, 4)  3.93 us
    unnamed x51, local copies, waits for them, and re-layouts  3.44 us
  transfers between devices with their start and end apart: 35, of which 14 were waited for; matrix products, arithmetic and copies ran while one was open for 11% of the time, Pallas kernels for 4%

commit v1 on v0

--- a/solution.py
+++ b/solution.py
@@ -356,10 +356,16 @@
     for s in range(1, rows_split):
         con.append(along(conduction_bands[0], s))
     info, route = tables(pair_list, transfer_index, owner_map, slots, groups, rows_split)
-    own = jnp.stack([bands] + [away(bands, 2 * k) for k in range(1, groups // 2)])
+    own = [bands]
+    for k in range(1, groups // 2):
+        own.append(away(bands, 2 * k))
+    own = jnp.stack(own)
     con_rest = jnp.concatenate(con, axis=0)
     con_rest, info, route = lax.optimization_barrier((con_rest, info, route))
-    own_rest = jnp.stack([con_rest] + [away(con_rest, 2 * k) for k in range(1, groups // 2)])
+    own_rest = [con_rest]
+    for k in range(1, groups // 2):
+        own_rest.append(away(con_rest, 2 * k))
+    own_rest = jnp.stack(own_rest)
     other = away(own, 1)
     other_rest = away(own_rest, 1)
 

time: 126 us -> 126 us (level)
  no operation moved by 1% of the time
where the time goes in v1:
time: 126 us; the launch traced here: 125 us
  starting transfers between devices  50.2 us (40%)
  waiting for transfers between devices  32.7 us (26%)
  Pallas kernels  24.7 us (20%)
  local copies, waits for them, and re-layouts  13.7 us (11%)
  other arithmetic  2.22 us (2%)
  between operations  1.74 us (1%)
    ppermute x23, starting transfers between devices, away(): return lax.ppermute(x, 'pb', [(i, i ^ k) for i in range(groups)])  30.9 us
    ppermute x23, waiting for transfers between devices, away(): return lax.ppermute(x, 'pb', [(i, i ^ k) for i in range(groups)])  19.8 us
    ppermute x12, starting transfers between devices, along(): return lax.ppermute(x, 'row', [(i, i ^ k) for i in range(rows_split)])  19.4 us
    pallas_call x2, Pallas kernels, pair_call(): pl.pallas_call(functools.partial(pair_body, slots=slots, rows_split=rows_...  15.4 us
    ppermute x12, waiting for transfers between devices, along(): return lax.ppermute(x, 'row', [(i, i ^ k) for i in range(rows_split)])  12.9 us
    another operation x8, local copies, waits for them, and re-layouts, step(): return mapped(valence_bands, conduction_bands, *rest)  5.2 us
    reshape x4, local copies, waits for them, and re-layouts, spread(): summed.reshape(per, nv, count, nc, nc).transpose(2, 0, 3, 1, 4)  3.93 us
    unnamed x51, local copies, waits for them, and re-layouts  3.44 us
  transfers between devices with their start and end apart: 35, of which 14 were waited for; matrix products, arithmetic and copies ran while one was open for 11% of the time, Pallas kernels for 4%

profile of v1, /device:TPU:0, one launch (start us, length us, event | category | flops | bytes accessed | tf_op | source)
XLA Modules:
  0.0 125.3 jit_solution(9391922442501987286)
XLA Ops:
  1.2 2.6 %collective-permute-start.10 = (bf16[20,1024]{1,0:T(8,128)(2,1)}, bf16[20,1024]{1,0:T(8,128)(2,1)S(1)}, u32[]{:S(2)}, u32[]{:S(2)}) collective-permute-start(bf16[20,1024]{1,0:T(8,128)(2,1)} %bitcast.30), channel_id=1, source_target_pairs={{0,1},{1,0},{2,3},{3,2},{4,5},{5,4},{6,7},{7,6},{8,9},{9,8},{10,11... | collective-permute-start | bytes 122888 | tf_op jit(solution)/shard_map/ppermute | solution.py:350
  3.9 2.6 %collective-permute-start.11 = (bf16[20,1024]{1,0:T(8,128)(2,1)}, bf16[20,1024]{1,0:T(8,128)(2,1)S(1)}, u32[]{:S(2)}, u32[]{:S(2)}) collective-permute-start(bf16[20,1024]{1,0:T(8,128)(2,1)} %bitcast.31), channel_id=1, source_target_pairs={{0,2},{1,3},{2,0},{3,1},{4,6},{5,7},{6,4},{7,5},{8,10},{9,11},{10,... | collective-permute-start | bytes 122888 | tf_op jit(solution)/shard_map/ppermute | solution.py:350
  6.4 2.3 %shard_map.77 = (s32[5,8]{1,0:T(8,128)S(1)}, s32[2,4,2]{2,1,0:T(4,128)}) custom-call(s32[2,16]{1,0:T(2,128)} %bitcast.41, s32[16]{0:T(128)} %bitcast.42, s32[8]{0:T(128)} %owners.1), custom_call_target="tpu_custom_call" | custom-call | tf_op jit(solution)/shard_map/pallas_call | solution.py:92
  8.7 1.4 %collective-permute-done.11 = bf16[20,1024]{1,0:T(8,128)(2,1)S(1)} collective-permute-done((bf16[20,1024]{1,0:T(8,128)(2,1)}, bf16[20,1024]{1,0:T(8,128)(2,1)S(1)}, u32[]{:S(2)}, u32[]{:S(2)}) %collective-permute-start.11) | collective-permute-done | bytes 40992 | tf_op jit(solution)/shard_map/ppermute | solution.py:350
  10.2 2.4 %collective-permute-done.12 = bf16[20,1024]{1,0:T(8,128)(2,1)S(1)} collective-permute-done((bf16[20,1024]{1,0:T(8,128)(2,1)}, bf16[20,1024]{1,0:T(8,128)(2,1)S(1)}, u32[]{:S(2)}, u32[]{:S(2)}) %collective-permute-start.12) | collective-permute-done | bytes 40992 | tf_op jit(solution)/shard_map/ppermute | solution.py:350
  12.6 1.6 %collective-permute-start.16 = (bf16[60,1024]{1,0:T(8,128)(2,1)S(1)}, bf16[60,1024]{1,0:T(8,128)(2,1)S(1)}, u32[]{:S(2)}, u32[]{:S(2)}) collective-permute-start(bf16[60,1024]{1,0:T(8,128)(2,1)S(1)} %pad_maximum_fusion.2), channel_id=1, source_target_pairs={{0,8},{4,12},{8,0},{12,4},{16,24},{20,28},{24,16},{28,20},{1,9},{5... | collective-permute-start | bytes 368648 | tf_op jit(solution)/shard_map/ppermute | solution.py:347
  14.1 1.5 %collective-permute-start.17 = (bf16[60,1024]{1,0:T(8,128)(2,1)S(1)}, bf16[60,1024]{1,0:T(8,128)(2,1)S(1)}, u32[]{:S(2)}, u32[]{:S(2)}) collective-permute-start(bf16[60,1024]{1,0:T(8,128)(2,1)S(1)} %pad_maximum_fusion.2), channel_id=1, source_target_pairs={{0,16},{4,20},{8,24},{12,28},{16,0},{20,4},{24,8},{28,12},{1,17},{... | collective-permute-start | bytes 368648 | tf_op jit(solution)/shard_map/ppermute | solution.py:347
  17.0 1.6 %collective-permute-start.13 = (bf16[40,1024]{1,0:T(8,128)(2,1)S(1)}, bf16[40,1024]{1,0:T(8,128)(2,1)S(1)}, u32[]{:S(2)}, u32[]{:S(2)}) collective-permute-start(bf16[40,1024]{1,0:T(8,128)(2,1)S(1)} %pad_maximum_fusion.3), channel_id=1, source_target_pairs={{0,8},{4,12},{8,0},{12,4},{16,24},{20,28},{24,16},{28,20},{1,9},{5... | collective-permute-start | bytes 245768 | tf_op jit(solution)/shard_map/ppermute | solution.py:347
  18.9 1.5 %collective-permute-start.14 = (bf16[40,1024]{1,0:T(8,128)(2,1)S(1)}, bf16[40,1024]{1,0:T(8,128)(2,1)S(1)}, u32[]{:S(2)}, u32[]{:S(2)}) collective-permute-start(bf16[40,1024]{1,0:T(8,128)(2,1)S(1)} %pad_maximum_fusion.3), channel_id=1, source_target_pairs={{0,16},{4,20},{8,24},{12,28},{16,0},{20,4},{24,8},{28,12},{1,17},{... | collective-permute-start | bytes 245768 | tf_op jit(solution)/shard_map/ppermute | solution.py:347
  20.4 3.1 %collective-permute-done.17 = bf16[60,1024]{1,0:T(8,128)(2,1)S(1)} collective-permute-done((bf16[60,1024]{1,0:T(8,128)(2,1)S(1)}, bf16[60,1024]{1,0:T(8,128)(2,1)S(1)}, u32[]{:S(2)}, u32[]{:S(2)}) %collective-permute-start.17) | collective-permute-done | bytes 122912 | tf_op jit(solution)/shard_map/ppermute | solution.py:347
  24.3 4.5 %collective-permute-done.15 = bf16[40,1024]{1,0:T(8,128)(2,1)S(1)} collective-permute-done((bf16[40,1024]{1,0:T(8,128)(2,1)S(1)}, bf16[40,1024]{1,0:T(8,128)(2,1)S(1)}, u32[]{:S(2)}, u32[]{:S(2)}) %collective-permute-start.15) | collective-permute-done | bytes 81952 | tf_op jit(solution)/shard_map/ppermute | solution.py:347
  30.6 13.7 %shard_map.78 = (bf16[100,800]{1,0:T(8,128)(2,1)}, bf16[100,800]{1,0:T(8,128)(2,1)}, bf16[100,800]{1,0:T(8,128)(2,1)}, bf16[100,800]{1,0:T(8,128)(2,1)}) custom-call(s32[5,8]{1,0:T(8,128)S(1)} %get-tuple-element.74.info, bf16[4,40,1024]{2,1,0:T(8,128)(2,1)S(1)} %pad_maximum_fusion.1.own, bf16[4,60,1024]{2,1,0:T(8,128)(2,1)S(1)} %pad_maximum_fusion.own_rest, ...), custom_call_target="tpu_custom_call" | custom-call | flops 6710886400 | bytes 8388608 | tf_op jit(solution)/shard_map/pallas_call | solution.py:231
  44.3 1.7 %shard_map.79 = (bf16[100,800]{1,0:T(8,128)(2,1)}, bf16[100,800]{1,0:T(8,128)(2,1)}, bf16[100,800]{1,0:T(8,128)(2,1)}, bf16[100,800]{1,0:T(8,128)(2,1)}) custom-call(s32[5,8]{1,0:T(8,128)S(1)} %get-tuple-element.74.info, bf16[4,40,1024]{2,1,0:T(8,128)(2,1)S(1)} %pad_maximum_fusion.1.own, bf16[4,60,1024]{2,1,0:T(8,128)(2,1)S(1)} %pad_maximum_fusion.own_rest, ...), custom_call_target="tpu_custom_call" | custom-call | flops 6710886400 | bytes 8388608 | tf_op jit(solution)/shard_map/pallas_call | solution.py:231
  46.1 5.2 %conditional.1 = (bf16[1,100,400]{2,1,0:T(8,128)(2,1)}, bf16[1,100,400]{2,1,0:T(8,128)(2,1)}, bf16[1,100,400]{2,1,0:T(8,128)(2,1)}, bf16[1,100,400]{2,1,0:T(8,12...) conditional(s32[]{:T(128)} %bitcast.15, () %tuple.21, ...), branch_computations={%region_0.0_spmd, %region_1.0_spmd} | conditional | flops 3355763200 | bytes 12469072 | solution.py:412
  51.4 1.7 %collective-permute-start.26 = (bf16[100,800]{1,0:T(8,128)(2,1)S(1)}, bf16[100,800]{1,0:T(8,128)(2,1)S(1)}, u32[]{:S(2)}, u32[]{:S(2)}) collective-permute-start(bf16[100,800]{1,0:T(8,128)(2,1)S(1)} %copy-done.24), channel_id=1, source_target_pairs={{0,2},{1,3},{2,0},{3,1},{4,6},{5,7},{6,4},{7,5},{8,10},{9,11},{10,... | collective-permute-start | bytes 480008 | tf_op jit(solution)/shard_map/ppermute | solution.py:350
  53.1 2.6 %collective-permute-start.27 = (bf16[100,800]{1,0:T(8,128)(2,1)S(1)}, bf16[100,800]{1,0:T(8,128)(2,1)S(1)}, u32[]{:S(2)}, u32[]{:S(2)}) collective-permute-start(bf16[100,800]{1,0:T(8,128)(2,1)S(1)} %copy-done.23), channel_id=1, source_target_pairs={{0,3},{1,2},{2,1},{3,0},{4,7},{5,6},{6,5},{7,4},{8,11},{9,10},{10,... | collective-permute-start | bytes 480008 | tf_op jit(solution)/shard_map/ppermute | solution.py:350
  55.7 1.8 %collective-permute-start.23 = (bf16[100,800]{1,0:T(8,128)(2,1)}, bf16[100,800]{1,0:T(8,128)(2,1)}, u32[]{:S(2)}, u32[]{:S(2)}) collective-permute-start(bf16[100,800]{1,0:T(8,128)(2,1)} %get-tuple-element.72), channel_id=1, source_target_pairs={{0,2},{1,3},{2,0},{3,1},{4,6},{5,7},{6,4},{7,5},{8,10},{9,11},{10,... | collective-permute-start | bytes 480008 | tf_op jit(solution)/shard_map/ppermute | solution.py:350
  57.5 2.6 %collective-permute-start.24 = (bf16[100,800]{1,0:T(8,128)(2,1)}, bf16[100,800]{1,0:T(8,128)(2,1)}, u32[]{:S(2)}, u32[]{:S(2)}) collective-permute-start(bf16[100,800]{1,0:T(8,128)(2,1)} %get-tuple-element.73), channel_id=1, source_target_pairs={{0,3},{1,2},{2,1},{3,0},{4,7},{5,6},{6,5},{7,4},{8,11},{9,10},{10,... | collective-permute-start | bytes 480008 | tf_op jit(solution)/shard_map/ppermute | solution.py:350
  60.1 8.3 %collective-permute-done.26 = bf16[100,800]{1,0:T(8,128)(2,1)S(1)} collective-permute-done((bf16[100,800]{1,0:T(8,128)(2,1)S(1)}, bf16[100,800]{1,0:T(8,128)(2,1)S(1)}, u32[]{:S(2)}, u32[]{:S(2)}) %collective-permute-start.26) | collective-permute-done | bytes 160032 | tf_op jit(solution)/shard_map/ppermute | solution.py:350
  68.5 1.3 %reshape.32 = bf16[5,20,2,20,20]{4,3,2,1,0:T(8,128)(2,1)S(1)} reshape(bf16[100,800]{1,0:T(8,128)(2,1)S(1)} %add_convert_fusion.1) | data formatting | bytes 320000 | tf_op jit(solution)/shard_map/reshape | solution.py:388
  70.9 12.6 %collective-permute-start.31 = (bf16[2,100,400]{2,1,0:T(8,128)(2,1)S(1)}, bf16[2,100,400]{2,1,0:T(8,128)(2,1)S(1)}, u32[]{:S(2)}, u32[]{:S(2)}) collective-permute-start(bf16[2,100,400]{2,1,0:T(8,128)(2,1)S(1)} %reshape.33.rest_1_), channel_id=1, source_target_pairs={{0,16},{4,20},{8,24},{12,28},{16,0},{20,4},{24,8},{28,12},{1,17},{... | collective-permute-start | bytes 480008 | tf_op jit(solution)/shard_map/ppermute | solution.py:347
  83.5 1.1 add_convert_fusion.2
  84.6 1.3 %reshape.30 = bf16[5,20,2,20,20]{4,3,2,1,0:T(8,128)(2,1)S(1)} reshape(bf16[100,800]{1,0:T(8,128)(2,1)S(1)} %add_convert_fusion.2) | data formatting | bytes 320000 | tf_op jit(solution)/shard_map/reshape | solution.py:388
  87.0 1.4 %collective-permute-start.28 = (bf16[2,100,400]{2,1,0:T(8,128)(2,1)S(1)}, bf16[2,100,400]{2,1,0:T(8,128)(2,1)S(1)}, u32[]{:S(2)}, u32[]{:S(2)}) collective-permute-start(bf16[2,100,400]{2,1,0:T(8,128)(2,1)S(1)} %reshape.31.rest_0_), channel_id=1, source_target_pairs={{0,8},{4,12},{8,0},{12,4},{16,24},{20,28},{24,16},{28,20},{1,9},{5... | collective-permute-start | bytes 480008 | tf_op jit(solution)/shard_map/ppermute | solution.py:347
  88.4 7.7 %collective-permute-start.30 = (bf16[2,100,400]{2,1,0:T(8,128)(2,1)S(1)}, bf16[2,100,400]{2,1,0:T(8,128)(2,1)S(1)}, u32[]{:S(2)}, u32[]{:S(2)}) collective-permute-start(bf16[2,100,400]{2,1,0:T(8,128)(2,1)S(1)} %reshape.31.rest_0_), channel_id=1, source_target_pairs={{0,16},{4,20},{8,24},{12,28},{16,0},{20,4},{24,8},{28,12},{1,17},{... | collective-permute-start | bytes 480008 | tf_op jit(solution)/shard_map/ppermute | solution.py:347
  96.8 9.5 %collective-permute-done.30.rest_6_ = bf16[2,100,400]{2,1,0:T(8,128)(2,1)S(1)} collective-permute-done((bf16[2,100,400]{2,1,0:T(8,128)(2,1)S(1)}, bf16[2,100,400]{2,1,0:T(8,128)(2,1)S(1)}, u32[]{:S(2)}, u32[]{:S(2)}) %collective-permute-start.30) | collective-permute-done | bytes 160032 | tf_op jit(solution)/shard_map/ppermute | solution.py:347
  109.7 2.5 %shard_map.81 = (bf16[2,100,100]{2,1,0:T(8,128)(2,1)}, bf16[2,100,100]{2,1,0:T(8,128)(2,1)}, bf16[2,100,100]{2,1,0:T(8,128)(2,1)}, bf16[2,100,100]{2,1,0:T(8,128)(2,1)}) custom-call(s32[2,4,2]{2,1,0:T(4,128)} %get-tuple-element.67.route, s32[5,8]{1,0:T(8,128)S(1)} %get-tuple-element.74.info, bf16[2,100,400]{2,1,0:T(8,128)(2,1)} %copy-done.1, ...), custom_call_target="tpu_custom_call" | custom-call | tf_op jit(solution)/shard_map/pallas_call | solution.py:303
  112.3 2.9 %collective-permute-start.42 = (bf16[2,100,100]{2,1,0:T(8,128)(2,1)}, bf16[2,100,100]{2,1,0:T(8,128)(2,1)S(1)}, u32[]{:S(2)}, u32[]{:S(2)}) collective-permute-start(bf16[2,100,100]{2,1,0:T(8,128)(2,1)} %get-tuple-element.100), channel_id=1, source_target_pairs={{0,1},{1,0},{2,3},{3,2},{4,5},{5,4},{6,7},{7,6},{8,9},{9,8},{10,11... | collective-permute-start | bytes 120008 | tf_op jit(solution)/shard_map/ppermute | solution.py:350
  115.6 2.0 %collective-permute-start.44 = (bf16[2,100,100]{2,1,0:T(8,128)(2,1)}, bf16[2,100,100]{2,1,0:T(8,128)(2,1)S(1)}, u32[]{:S(2)}, u32[]{:S(2)}) collective-permute-start(bf16[2,100,100]{2,1,0:T(8,128)(2,1)} %get-tuple-element.102), channel_id=1, source_target_pairs={{0,3},{1,2},{2,1},{3,0},{4,7},{5,6},{6,5},{7,4},{8,11},{9,10},{10,... | collective-permute-start | bytes 120008 | tf_op jit(solution)/shard_map/ppermute | solution.py:350
  117.6 2.4 %shard_map.80 = bf16[2,100,400]{2,1,0:T(8,128)(2,1)} custom-call(s32[2,4,2]{2,1,0:T(4,128)} %get-tuple-element.67.route, bf16[2,100,400]{2,1,0:T(8,128)(2,1)} %copy-done.1, bf16[2,100,400]{2,1,0:T(8,128)(2,1)} %copy-done, bf16[1,100,400]{2,1,0:T(8,128)(2,1)} %get-tuple-element.91.rest_2_, bf16[2,100,400]{2,1,0:T(8,128)(2,1)} %copy-done.5, ...), custom_call_target="tpu_custom_call" | custom-call | tf_op jit(solution)/shard_map/pallas_call | solution.py:275
  120.1 1.8 %copy.15 = bf16[2,100,400]{2,0,1:T(2,128)(2,1)} copy(bf16[2,100,400]{2,1,0:T(8,128)(2,1)} %shard_map.80) | data formatting | bytes 320000
  123.3 2.0 %shard_map.82 = bf16[100,2,400]{2,1,0:T(2,128)(2,1)} custom-call(s32[5,8]{1,0:T(8,128)S(1)} %get-tuple-element.74.info, bf16[2,100,100]{2,1,0:T(8,128)(2,1)} %get-tuple-element.99.rest_0_, bf16[2,100,100]{2,1,0:T(8,128)(2,1)} %copy-done.19, bf16[2,100,100]{2,1,0:T(8,128)(2,1)} %copy-done.20, bf16[2,100,100]{2,1,0:T(8,128)(2,1)} %copy-done.21), custom_call_target="tpu_custom_call" | custom-call | tf_op jit(solution)/shard_map/pallas_call | solution.py:329
  (118 shorter events, 17.6 us)
Async XLA Ops:
  0.7 29.9 %collective-permute-start.21 = (bf16[1024,4096]{1,0:T(8,128)(2,1)}, bf16[1024,4096]{1,0:T(8,128)(2,1)}, u32[]{:S(2)}, u32[]{:S(2)}) collective-permute-start(bf16[1024,4096]{1,0:T(8,128)(2,1)} %bitcast.19), channel_id=1, source_target_pairs={{0,4},{4,0},{8,12},{12,8},{16,20},{20,16},{24,28},{28,24},{1,5},{5... | collective-permute-start | bytes 25165832 | tf_op jit(solution)/shard_map/ppermute | solution.py:347
  1.2 7.5 %collective-permute-start.10 = (bf16[20,1024]{1,0:T(8,128)(2,1)}, bf16[20,1024]{1,0:T(8,128)(2,1)S(1)}, u32[]{:S(2)}, u32[]{:S(2)}) collective-permute-start(bf16[20,1024]{1,0:T(8,128)(2,1)} %bitcast.30), channel_id=1, source_target_pairs={{0,1},{1,0},{2,3},{3,2},{4,5},{5,4},{6,7},{7,6},{8,9},{9,8},{10,11... | collective-permute-start | bytes 122888 | tf_op jit(solution)/shard_map/ppermute | solution.py:350
  3.9 6.3 %collective-permute-start.11 = (bf16[20,1024]{1,0:T(8,128)(2,1)}, bf16[20,1024]{1,0:T(8,128)(2,1)S(1)}, u32[]{:S(2)}, u32[]{:S(2)}) collective-permute-start(bf16[20,1024]{1,0:T(8,128)(2,1)} %bitcast.31), channel_id=1, source_target_pairs={{0,2},{1,3},{2,0},{3,1},{4,6},{5,7},{6,4},{7,5},{8,10},{9,11},{10,... | collective-permute-start | bytes 122888 | tf_op jit(solution)/shard_map/ppermute | solution.py:350
  6.4 6.1 %collective-permute-start.12 = (bf16[20,1024]{1,0:T(8,128)(2,1)}, bf16[20,1024]{1,0:T(8,128)(2,1)S(1)}, u32[]{:S(2)}, u32[]{:S(2)}) collective-permute-start(bf16[20,1024]{1,0:T(8,128)(2,1)} %bitcast.32), channel_id=1, source_target_pairs={{0,3},{1,2},{2,1},{3,0},{4,7},{5,6},{6,5},{7,4},{8,11},{9,10},{10,... | collective-permute-start | bytes 122888 | tf_op jit(solution)/shard_map/ppermute | solution.py:350
  12.6 6.3 %collective-permute-start.16 = (bf16[60,1024]{1,0:T(8,128)(2,1)S(1)}, bf16[60,1024]{1,0:T(8,128)(2,1)S(1)}, u32[]{:S(2)}, u32[]{:S(2)}) collective-permute-start(bf16[60,1024]{1,0:T(8,128)(2,1)S(1)} %pad_maximum_fusion.2), channel_id=1, source_target_pairs={{0,8},{4,12},{8,0},{12,4},{16,24},{20,28},{24,16},{28,20},{1,9},{5... | collective-permute-start | bytes 368648 | tf_op jit(solution)/shard_map/ppermute | solution.py:347
  14.1 9.3 %collective-permute-start.17 = (bf16[60,1024]{1,0:T(8,128)(2,1)S(1)}, bf16[60,1024]{1,0:T(8,128)(2,1)S(1)}, u32[]{:S(2)}, u32[]{:S(2)}) collective-permute-start(bf16[60,1024]{1,0:T(8,128)(2,1)S(1)} %pad_maximum_fusion.2), channel_id=1, source_target_pairs={{0,16},{4,20},{8,24},{12,28},{16,0},{20,4},{24,8},{28,12},{1,17},{... | collective-permute-start | bytes 368648 | tf_op jit(solution)/shard_map/ppermute | solution.py:347
  15.7 7.8 %collective-permute-start.18 = (bf16[60,1024]{1,0:T(8,128)(2,1)S(1)}, bf16[60,1024]{1,0:T(8,128)(2,1)S(1)}, u32[]{:S(2)}, u32[]{:S(2)}) collective-permute-start(bf16[60,1024]{1,0:T(8,128)(2,1)S(1)} %pad_maximum_fusion.2), channel_id=1, source_target_pairs={{0,24},{4,28},{8,16},{12,20},{16,8},{20,12},{24,0},{28,4},{1,25},{... | collective-permute-start | bytes 368648 | tf_op jit(solution)/shard_map/ppermute | solution.py:347
  17.0 6.7 %collective-permute-start.13 = (bf16[40,1024]{1,0:T(8,128)(2,1)S(1)}, bf16[40,1024]{1,0:T(8,128)(2,1)S(1)}, u32[]{:S(2)}, u32[]{:S(2)}) collective-permute-start(bf16[40,1024]{1,0:T(8,128)(2,1)S(1)} %pad_maximum_fusion.3), channel_id=1, source_target_pairs={{0,8},{4,12},{8,0},{12,4},{16,24},{20,28},{24,16},{28,20},{1,9},{5... | collective-permute-start | bytes 245768 | tf_op jit(solution)/shard_map/ppermute | solution.py:347
  18.9 5.5 %collective-permute-start.14 = (bf16[40,1024]{1,0:T(8,128)(2,1)S(1)}, bf16[40,1024]{1,0:T(8,128)(2,1)S(1)}, u32[]{:S(2)}, u32[]{:S(2)}) collective-permute-start(bf16[40,1024]{1,0:T(8,128)(2,1)S(1)} %pad_maximum_fusion.3), channel_id=1, source_target_pairs={{0,16},{4,20},{8,24},{12,28},{16,0},{20,4},{24,8},{28,12},{1,17},{... | collective-permute-start | bytes 245768 | tf_op jit(solution)/shard_map/ppermute | solution.py:347
  23.5 5.3 %collective-permute-start.15 = (bf16[40,1024]{1,0:T(8,128)(2,1)S(1)}, bf16[40,1024]{1,0:T(8,128)(2,1)S(1)}, u32[]{:S(2)}, u32[]{:S(2)}) collective-permute-start(bf16[40,1024]{1,0:T(8,128)(2,1)S(1)} %pad_maximum_fusion.3), channel_id=1, source_target_pairs={{0,24},{4,28},{8,16},{12,20},{16,8},{20,12},{24,0},{28,4},{1,25},{... | collective-permute-start | bytes 245768 | tf_op jit(solution)/shard_map/ppermute | solution.py:347
  23.6 7.0 %collective-permute-start.20 = (bf16[4,60,1024]{2,1,0:T(8,128)(2,1)S(1)}, bf16[4,60,1024]{2,1,0:T(8,128)(2,1)S(1)}, u32[]{:S(2)}, u32[]{:S(2)}) collective-permute-start(bf16[4,60,1024]{2,1,0:T(8,128)(2,1)S(1)} %pad_maximum_fusion.own_rest), channel_id=1, source_target_pairs={{0,4},{4,0},{8,12},{12,8},{16,20},{20,16},{24,28},{28,24},{1,5},{5... | collective-permute-start | bytes 1474568 | tf_op jit(solution)/shard_map/ppermute | solution.py:347
  46.0 11.5 %collective-permute-start.25 = (bf16[100,800]{1,0:T(8,128)(2,1)}, bf16[100,800]{1,0:T(8,128)(2,1)S(1)}, u32[]{:S(2)}, u32[]{:S(2)}) collective-permute-start(bf16[100,800]{1,0:T(8,128)(2,1)} %get-tuple-element.76), channel_id=1, source_target_pairs={{0,1},{1,0},{2,3},{3,2},{4,5},{5,4},{6,7},{7,6},{8,9},{9,8},{10,11... | collective-permute-start | bytes 480008 | tf_op jit(solution)/shard_map/ppermute | solution.py:350
  51.4 17.0 %collective-permute-start.26 = (bf16[100,800]{1,0:T(8,128)(2,1)S(1)}, bf16[100,800]{1,0:T(8,128)(2,1)S(1)}, u32[]{:S(2)}, u32[]{:S(2)}) collective-permute-start(bf16[100,800]{1,0:T(8,128)(2,1)S(1)} %copy-done.24), channel_id=1, source_target_pairs={{0,2},{1,3},{2,0},{3,1},{4,6},{5,7},{6,4},{7,5},{8,10},{9,11},{10,... | collective-permute-start | bytes 480008 | tf_op jit(solution)/shard_map/ppermute | solution.py:350
  53.1 15.3 %collective-permute-start.27 = (bf16[100,800]{1,0:T(8,128)(2,1)S(1)}, bf16[100,800]{1,0:T(8,128)(2,1)S(1)}, u32[]{:S(2)}, u32[]{:S(2)}) collective-permute-start(bf16[100,800]{1,0:T(8,128)(2,1)S(1)} %copy-done.23), channel_id=1, source_target_pairs={{0,3},{1,2},{2,1},{3,0},{4,7},{5,6},{6,5},{7,4},{8,11},{9,10},{10,... | collective-permute-start | bytes 480008 | tf_op jit(solution)/shard_map/ppermute | solution.py:350
  55.7 27.7 %collective-permute-start.22 = (bf16[100,800]{1,0:T(8,128)(2,1)S(1)}, bf16[100,800]{1,0:T(8,128)(2,1)S(1)}, u32[]{:S(2)}, u32[]{:S(2)}) collective-permute-start(bf16[100,800]{1,0:T(8,128)(2,1)S(1)} %copy-done.22), channel_id=1, source_target_pairs={{0,1},{1,0},{2,3},{3,2},{4,5},{5,4},{6,7},{7,6},{8,9},{9,8},{10,11... | collective-permute-start | bytes 480008 | tf_op jit(solution)/shard_map/ppermute | solution.py:350
  55.7 27.7 %collective-permute-start.23 = (bf16[100,800]{1,0:T(8,128)(2,1)}, bf16[100,800]{1,0:T(8,128)(2,1)}, u32[]{:S(2)}, u32[]{:S(2)}) collective-permute-start(bf16[100,800]{1,0:T(8,128)(2,1)} %get-tuple-element.72), channel_id=1, source_target_pairs={{0,2},{1,3},{2,0},{3,1},{4,6},{5,7},{6,4},{7,5},{8,10},{9,11},{10,... | collective-permute-start | bytes 480008 | tf_op jit(solution)/shard_map/ppermute | solution.py:350
  57.5 26.0 %collective-permute-start.24 = (bf16[100,800]{1,0:T(8,128)(2,1)}, bf16[100,800]{1,0:T(8,128)(2,1)}, u32[]{:S(2)}, u32[]{:S(2)}) collective-permute-start(bf16[100,800]{1,0:T(8,128)(2,1)} %get-tuple-element.73), channel_id=1, source_target_pairs={{0,3},{1,2},{2,1},{3,0},{4,7},{5,6},{6,5},{7,4},{8,11},{9,10},{10,... | collective-permute-start | bytes 480008 | tf_op jit(solution)/shard_map/ppermute | solution.py:350
  70.8 17.6 %collective-permute-start.29 = (bf16[2,100,400]{2,1,0:T(8,128)(2,1)S(1)}, bf16[2,100,400]{2,1,0:T(8,128)(2,1)S(1)}, u32[]{:S(2)}, u32[]{:S(2)}) collective-permute-start(bf16[2,100,400]{2,1,0:T(8,128)(2,1)S(1)} %reshape.33.rest_1_), channel_id=1, source_target_pairs={{0,8},{4,12},{8,0},{12,4},{16,24},{20,28},{24,16},{28,20},{1,9},{5... | collective-permute-start | bytes 480008 | tf_op jit(solution)/shard_map/ppermute | solution.py:347
  70.9 25.3 %collective-permute-start.31 = (bf16[2,100,400]{2,1,0:T(8,128)(2,1)S(1)}, bf16[2,100,400]{2,1,0:T(8,128)(2,1)S(1)}, u32[]{:S(2)}, u32[]{:S(2)}) collective-permute-start(bf16[2,100,400]{2,1,0:T(8,128)(2,1)S(1)} %reshape.33.rest_1_), channel_id=1, source_target_pairs={{0,16},{4,20},{8,24},{12,28},{16,0},{20,4},{24,8},{28,12},{1,17},{... | collective-permute-start | bytes 480008 | tf_op jit(solution)/shard_map/ppermute | solution.py:347
  83.4 12.7 %collective-permute-start.33 = (bf16[2,100,400]{2,1,0:T(8,128)(2,1)S(1)}, bf16[2,100,400]{2,1,0:T(8,128)(2,1)S(1)}, u32[]{:S(2)}, u32[]{:S(2)}) collective-permute-start(bf16[2,100,400]{2,1,0:T(8,128)(2,1)S(1)} %reshape.33.rest_1_), channel_id=1, source_target_pairs={{0,24},{4,28},{8,16},{12,20},{16,8},{20,12},{24,0},{28,4},{1,25},{... | collective-permute-start | bytes 480008 | tf_op jit(solution)/shard_map/ppermute | solution.py:347
  83.4 12.8 %collective-permute-start.35 = (bf16[2,100,400]{2,1,0:T(8,128)(2,1)S(1)}, bf16[2,100,400]{2,1,0:T(8,128)(2,1)}, u32[]{:S(2)}, u32[]{:S(2)}) collective-permute-start(bf16[2,100,400]{2,1,0:T(8,128)(2,1)S(1)} %reshape.33.rest_1_), channel_id=1, source_target_pairs={{0,4},{4,0},{8,12},{12,8},{16,20},{20,16},{24,28},{28,24},{1,5},{5... | collective-permute-start | bytes 480008 | tf_op jit(solution)/shard_map/ppermute | solution.py:347
  87.0 9.8 %collective-permute-start.28 = (bf16[2,100,400]{2,1,0:T(8,128)(2,1)S(1)}, bf16[2,100,400]{2,1,0:T(8,128)(2,1)S(1)}, u32[]{:S(2)}, u32[]{:S(2)}) collective-permute-start(bf16[2,100,400]{2,1,0:T(8,128)(2,1)S(1)} %reshape.31.rest_0_), channel_id=1, source_target_pairs={{0,8},{4,12},{8,0},{12,4},{16,24},{20,28},{24,16},{28,20},{1,9},{5... | collective-permute-start | bytes 480008 | tf_op jit(solution)/shard_map/ppermute | solution.py:347
  88.4 17.9 %collective-permute-start.30 = (bf16[2,100,400]{2,1,0:T(8,128)(2,1)S(1)}, bf16[2,100,400]{2,1,0:T(8,128)(2,1)S(1)}, u32[]{:S(2)}, u32[]{:S(2)}) collective-permute-start(bf16[2,100,400]{2,1,0:T(8,128)(2,1)S(1)} %reshape.31.rest_0_), channel_id=1, source_target_pairs={{0,16},{4,20},{8,24},{12,28},{16,0},{20,4},{24,8},{28,12},{1,17},{... | collective-permute-start | bytes 480008 | tf_op jit(solution)/shard_map/ppermute | solution.py:347
  96.1 10.2 %collective-permute-start.32 = (bf16[2,100,400]{2,1,0:T(8,128)(2,1)S(1)}, bf16[2,100,400]{2,1,0:T(8,128)(2,1)S(1)}, u32[]{:S(2)}, u32[]{:S(2)}) collective-permute-start(bf16[2,100,400]{2,1,0:T(8,128)(2,1)S(1)} %reshape.31.rest_0_), channel_id=1, source_target_pairs={{0,24},{4,28},{8,16},{12,20},{16,8},{20,12},{24,0},{28,4},{1,25},{... | collective-permute-start | bytes 480008 | tf_op jit(solution)/shard_map/ppermute | solution.py:347
  96.1 10.7 %collective-permute-start.34 = (bf16[2,100,400]{2,1,0:T(8,128)(2,1)S(1)}, bf16[2,100,400]{2,1,0:T(8,128)(2,1)S(1)}, u32[]{:S(2)}, u32[]{:S(2)}) collective-permute-start(bf16[2,100,400]{2,1,0:T(8,128)(2,1)S(1)} %reshape.31.rest_0_), channel_id=1, source_target_pairs={{0,4},{4,0},{8,12},{12,8},{16,20},{20,16},{24,28},{28,24},{1,5},{5... | collective-permute-start | bytes 480008 | tf_op jit(solution)/shard_map/ppermute | solution.py:347
  96.2 10.7 %collective-permute-start.37 = (bf16[2,100,400]{2,1,0:T(8,128)(2,1)S(1)}, bf16[2,100,400]{2,1,0:T(8,128)(2,1)S(1)}, u32[]{:S(2)}, u32[]{:S(2)}) collective-permute-start(bf16[2,100,400]{2,1,0:T(8,128)(2,1)S(1)} %collective-permute-done.29.rest_4_), channel_id=1, source_target_pairs={{0,4},{4,0},{8,12},{12,8},{16,20},{20,16},{24,28},{28,24},{1,5},{5... | collective-permute-start | bytes 480008 | tf_op jit(solution)/shard_map/ppermute | solution.py:347
  96.7 10.6 %collective-permute-start.39 = (bf16[2,100,400]{2,1,0:T(8,128)(2,1)S(1)}, bf16[2,100,400]{2,1,0:T(8,128)(2,1)S(1)}, u32[]{:S(2)}, u32[]{:S(2)}) collective-permute-start(bf16[2,100,400]{2,1,0:T(8,128)(2,1)S(1)} %collective-permute-done.31.rest_7_), channel_id=1, source_target_pairs={{0,4},{4,0},{8,12},{12,8},{16,20},{20,16},{24,28},{28,24},{1,5},{5... | collective-permute-start | bytes 480008 | tf_op jit(solution)/shard_map/ppermute | solution.py:347
  106.3 1.8 %collective-permute-start.36 = (bf16[2,100,400]{2,1,0:T(8,128)(2,1)S(1)}, bf16[2,100,400]{2,1,0:T(8,128)(2,1)S(1)}, u32[]{:S(2)}, u32[]{:S(2)}) collective-permute-start(bf16[2,100,400]{2,1,0:T(8,128)(2,1)S(1)} %collective-permute-done.28.rest_3_), channel_id=1, source_target_pairs={{0,4},{4,0},{8,12},{12,8},{16,20},{20,16},{24,28},{28,24},{1,5},{5... | collective-permute-start | bytes 480008 | tf_op jit(solution)/shard_map/ppermute | solution.py:347
  106.9 1.8 %collective-permute-start.40 = (bf16[2,100,400]{2,1,0:T(8,128)(2,1)S(1)}, bf16[2,100,400]{2,1,0:T(8,128)(2,1)S(1)}, u32[]{:S(2)}, u32[]{:S(2)}) collective-permute-start(bf16[2,100,400]{2,1,0:T(8,128)(2,1)S(1)} %collective-permute-done.32.rest_9_), channel_id=1, source_target_pairs={{0,4},{4,0},{8,12},{12,8},{16,20},{20,16},{24,28},{28,24},{1,5},{5... | collective-permute-start | bytes 480008 | tf_op jit(solution)/shard_map/ppermute | solution.py:347
  112.3 9.5 %collective-permute-start.42 = (bf16[2,100,100]{2,1,0:T(8,128)(2,1)}, bf16[2,100,100]{2,1,0:T(8,128)(2,1)S(1)}, u32[]{:S(2)}, u32[]{:S(2)}) collective-permute-start(bf16[2,100,100]{2,1,0:T(8,128)(2,1)} %get-tuple-element.100), channel_id=1, source_target_pairs={{0,1},{1,0},{2,3},{3,2},{4,5},{5,4},{6,7},{7,6},{8,9},{9,8},{10,11... | collective-permute-start | bytes 120008 | tf_op jit(solution)/shard_map/ppermute | solution.py:350
  115.2 7.5 %collective-permute-start.43 = (bf16[2,100,100]{2,1,0:T(8,128)(2,1)}, bf16[2,100,100]{2,1,0:T(8,128)(2,1)S(1)}, u32[]{:S(2)}, u32[]{:S(2)}) collective-permute-start(bf16[2,100,100]{2,1,0:T(8,128)(2,1)} %get-tuple-element.101), channel_id=1, source_target_pairs={{0,2},{1,3},{2,0},{3,1},{4,6},{5,7},{6,4},{7,5},{8,10},{9,11},{10,... | collective-permute-start | bytes 120008 | tf_op jit(solution)/shard_map/ppermute | solution.py:350
  115.6 7.0 %collective-permute-start.44 = (bf16[2,100,100]{2,1,0:T(8,128)(2,1)}, bf16[2,100,100]{2,1,0:T(8,128)(2,1)S(1)}, u32[]{:S(2)}, u32[]{:S(2)}) collective-permute-start(bf16[2,100,100]{2,1,0:T(8,128)(2,1)} %get-tuple-element.102), channel_id=1, source_target_pairs={{0,3},{1,2},{2,1},{3,0},{4,7},{5,6},{6,5},{7,4},{8,11},{9,10},{10,... | collective-permute-start | bytes 120008 | tf_op jit(solution)/shard_map/ppermute | solution.py:350
  (28 other events, 218.1 us)
